TPU v7x, 256 devices: a whole 4x4x8 slice. The times are simulated.
256 devices in a mesh: row: 16 (over z, core), col: 16 (over x, y).
Axes of the slice: x: 4, y: 4, z: 8, core: 2. Of those that a mesh axis runs over, the one named last changes fastest.
Arguments:
- token_ids: int32 [32, 256], P('row'), may hold values from 0 to 16383
- passage_lengths: int32 [32], P('row'), may hold values from 64 to 256, as said below
- embedding: bfloat16 [16384, 4096], P(None, 'col'), may hold values from -8 to 8
- attn_gain: bfloat16 [4096], P('col'), may hold values from 0.25 to 1.75
- final_gain: bfloat16 [4096], P('col'), may hold values from 0.25 to 1.75
- query_weight: bfloat16 [4096, 4096], P('row', 'col'), may hold values from -0.5 to 0.5
- key_weight: bfloat16 [4096, 4096], P('row', 'col'), may hold values from -0.5 to 0.5
- value_weight: bfloat16 [4096, 4096], P('row', 'col'), may hold values from -0.09375 to 0.09375
- out_weight: bfloat16 [4096, 4096], P('row', 'col'), may hold values from -0.09375 to 0.09375
- crosskey_weight: bfloat16 [4096, 4096], P('row', 'col'), may hold values from -0.09375 to 0.09375
- crossvalue_weight: bfloat16 [4096, 4096], P('row', 'col'), may hold values from -0.09375 to 0.09375
Outputs:
- hidden_out: bfloat16 [8192, 4096], P('row', 'col')
- cross_keys: bfloat16 [8192, 16, 256], P('row', 'col')
- cross_values: bfloat16 [8192, 16, 256], P('row', 'col')
Inputs may be any that keep to these rules, and one draw needn't show every extreme that they name: `passage_lengths`: some passage of every draw has all 256 slots valid.
All inputs are finite; a program needn't handle non-finite values.
Results may differ from a plain program's by a relative error of at most 0.0082.
Values may be sent and summed in bfloat16 or wider, within the bound.
No kernel may reach another device: no remote copies, remote signals or barrier semaphores. Data moves between devices by JAX's collectives and lax.ppermute only.
A program may use at most 64 MiB of HBM per device.

v0:
```python
import jax
import jax.numpy as jnp
from jax import lax
from jax.experimental import pallas as pl
from jax.experimental.pallas import tpu as pltpu
from jax.sharding import PartitionSpec as P

D = 4096
HD = 256
PLEN = 256
SIDE = 4
BLOCKS = SIDE * SIDE
GAIN_ROWS = 16

epsilon = 1e-06
masked_score = -1000000000.0


ANY = pl.BlockSpec(memory_space=pl.ANY)
SMEM = pl.BlockSpec(memory_space=pltpu.SMEM)
VMEM = pl.BlockSpec(memory_space=pltpu.VMEM)
HBM = pl.BlockSpec(memory_space=pltpu.HBM)

DEPTH = 8
SHIFTS = (1, 3, 2)
OFFSETS = (0, 3, 1, 2)


def moves(step):
    def index(z, c, x, y):
        return ((z % DEPTH * 2 + c) * SIDE + x % SIDE) * SIDE + y % SIDE

    return [
        (index(z, c, x, y), index(*step(z, c, x, y)))
        for z in range(DEPTH)
        for c in range(2)
        for x in range(SIDE)
        for y in range(SIDE)
    ]


def send(block, step):
    return lax.ppermute(block, ("row", "col"), moves(step))


def first_leg(block, shift):
    return send(block, lambda z, c, x, y: (z, c, x + shift * (1 - c), y + shift * c))


def second_leg(block, shift):
    return send(block, lambda z, c, x, y: (z, c, x + shift * c, y + shift * (1 - c)))


def along_z(block):
    return send(block, lambda z, c, x, y: (z + 1 - 2 * c, c, x, y))


def swap_cores(block):
    return send(block, lambda z, c, x, y: (z, 1 - c, x, y))


def gather_first(chunk):
    return jnp.stack([chunk] + [first_leg(chunk, s) for s in SHIFTS])


def gather_direct(chunk):
    stack = gather_first(chunk)
    return [stack] + [second_leg(stack, s) for s in SHIFTS]


def gather_halved(chunk):
    stack = gather_first(chunk)
    back, ahead = second_leg(stack, 1), second_leg(stack, 3)
    return [stack, back, ahead, second_leg(back[:2], 1), second_leg(ahead[2:], 3)]


def gather_weight(shard, other, late):
    block = jnp.stack([shard, other])
    parts = [shard, other]
    hops = []
    for hop in range(1, DEPTH // 2 + 1):
        block = along_z(block if hop < DEPTH // 2 else block[0])
        hops.append(block)
    if late:
        both = jnp.concatenate(hops[:3] + [hops[3][None]])
        return parts + hops + [swap_cores(both)]
    crossed = swap_cores(jnp.concatenate(hops[:3]))
    return parts + hops + [crossed, swap_cores(hops[3])]


def arrival(place, row):
    z, c = place[0], place[1]
    away = lax.rem((lax.div(row, 2) - z) * (1 - 2 * c) + DEPTH, DEPTH)
    same = jnp.where(lax.rem(row, 2) == c, 1, 0)
    near = jnp.where(away == 0, 1 - same, 14 + 1 - same)
    behind = 2 + 2 * (DEPTH - 1 - away) + 1 - same
    ahead = 8 + 2 * (away - 1) + same
    half = DEPTH // 2
    inner = jnp.where(away > half, behind, ahead)
    return jnp.where((away == 0) | (away == half), near, inner)


def late_places(place):
    z, c = place[0], place[1]
    up = 1 - 2 * c

    def row(depth, core):
        return lax.rem(depth + DEPTH, DEPTH) * 2 + core

    last = DEPTH // 2
    places = [(0, None, row(z, c)), (1, None, row(z, 1 - c))]
    for hop in range(1, last):
        places += [(1 + hop, 0, row(z - hop * up, c)), (1 + hop, 1, row(z - hop * up, 1 - c))]
        spot = 2 * hop - 2
        places += [(6, spot, row(z + hop * up, 1 - c)), (6, spot + 1, row(z + hop * up, c))]
    return places + [(5, None, row(z + last, c)), (6, 6, row(z + last, 1 - c))]


def gather_spot(place, row):
    c = place[1]
    away_x = lax.rem(lax.div(row, SIDE) - place[2] + SIDE, SIDE)
    away_y = lax.rem(lax.rem(row, SIDE) - place[3] + SIDE, SIDE)

    def index(away):
        return jnp.where(away == 0, 0, jnp.where(away == 3, 1, away + 1))

    first = index(away_x * (1 - c) + away_y * c)
    second = index(away_x * c + away_y * (1 - c))
    return second * SIDE + first


def block_of(place, first, second):
    c = place[1]
    x = place[2] + OFFSETS[first] * (1 - c) + OFFSETS[second] * c
    y = place[3] + OFFSETS[first] * c + OFFSETS[second] * (1 - c)
    return lax.rem(x, SIDE) * SIDE + lax.rem(y, SIDE)


def read(place_ref):
    row, col = place_ref[0], place_ref[1]
    return [lax.div(row, 2), lax.rem(row, 2), lax.div(col, SIDE), lax.rem(col, SIDE)]


def start_all(copies):
    for copy in copies:
        copy.start()


def wait_all(copies):
    for copy in copies:
        copy.wait()


def lanes(square):
    return sum(square[:, n * 128 : (n + 1) * 128] for n in range(square.shape[1] // 128))


def prepare_kernel(place_ref, own, back, ahead, far, rows, square, final_ref):
    place = read(place_ref)
    tokens, step = rows.shape[0], 64
    for second, part in enumerate((own, back, ahead, far)):
        for first in range(SIDE):
            spot = arrival(place, block_of(place, first, second))
            there = pl.ds(pl.multiple_of(spot * HD, HD), HD)
            gains = part[first, pl.ds(tokens, GAIN_ROWS), :].astype(jnp.float32)
            final_ref[second * SIDE + first] = gains[1:2, :]
            gain = gains[0:1, :]

            @pl.loop(0, tokens // step)
            def _(tile):
                here = pl.ds(pl.multiple_of(tile * step, step), step)
                wide = part[first, here, :].astype(jnp.float32)
                total = lanes(wide * wide)
                square[here, :] = total if second + first == 0 else square[here, :] + total
                rows[here, there] = (wide * gain).astype(jnp.bfloat16)


def weight_loads(sources, held, sem):
    copies, at = [], 0
    for n, source in enumerate(sources):
        if len(source.shape) == 2:
            copies.append(pltpu.make_async_copy(source, held.at[at], sem.at[n]))
            at += 1
        else:
            count = source.shape[0]
            copies.append(pltpu.make_async_copy(source, held.at[pl.ds(at, count)], sem.at[n]))
            at += count
    return copies


def project_kernel(rows, own, other, hop1, hop2, hop3, crossed, total, held, sem):
    copies = weight_loads((own, other, hop1, hop2, hop3, crossed), held, sem)
    start_all(copies)
    wait_all(copies)
    weight = held.reshape(14 * HD, 3 * HD)

    @pl.loop(0, 6)
    def _(n):
        here = pl.ds(pl.multiple_of(lax.div(n, 3) * PLEN, PLEN), PLEN)
        there = pl.ds(pl.multiple_of(lax.rem(n, 3) * HD, HD), HD)
        total[here, there] = jnp.dot(
            rows[here, : 14 * HD], weight[:, there], preferred_element_type=jnp.float32
        )


def attend_kernel(len_ref, rows, square, total, far, far_crossed, out, heads):
    @pl.loop(0, 2)
    def _(p):
        here = pl.ds(pl.multiple_of(p * PLEN, PLEN), PLEN)
        mean = jnp.sum(square[here, :], axis=1, keepdims=True) / D
        inverse = lax.rsqrt(mean + epsilon)
        for n in range(3):
            there = pl.ds(n * HD, HD)
            head = total[here, there]
            head += jnp.dot(rows[here, 14 * HD : 15 * HD], far[:, there], preferred_element_type=jnp.float32)
            head += jnp.dot(rows[here, 15 * HD :], far_crossed[:, there], preferred_element_type=jnp.float32)
            heads[n] = (head * inverse).astype(jnp.bfloat16)
        scores = lax.dot_general(
            heads[0], heads[1], (((1,), (1,)), ((), ())), preferred_element_type=jnp.float32
        ) * HD ** (-0.5)
        slot = lax.broadcasted_iota(jnp.int32, (PLEN, PLEN), 1)
        scores = jnp.where(slot < len_ref[p], scores, masked_score)
        expon = jnp.exp(scores - jnp.max(scores, axis=-1, keepdims=True))
        probs = (expon / jnp.sum(expon, axis=-1, keepdims=True)).astype(jnp.bfloat16)
        out[here, :] = jnp.dot(probs, heads[2], preferred_element_type=jnp.float32).astype(jnp.bfloat16)


def arrange_kernel(*refs):
    place = read(refs[0])
    parts, out, sem = refs[1:8], refs[8], refs[9]
    copies = []
    for n, (part, spot, row) in enumerate(late_places(place)):
        source = parts[part] if spot is None else parts[part].at[spot]
        copies.append(pltpu.make_async_copy(source, out.at[gather_spot(place, row)], sem.at[n]))
    start_all(copies)
    wait_all(copies)


def residual_near_kernel(own, back, ahead, weight, embedded, total):
    @pl.loop(0, 2)
    def _(p):
        here = pl.ds(pl.multiple_of(p * PLEN, PLEN), PLEN)
        sum_here = embedded[here, :].astype(jnp.float32)
        for k in range(12):
            part = (own, back, ahead)[k // SIDE]
            sum_here += jnp.dot(part[k % SIDE, here, :], weight[k], preferred_element_type=jnp.float32)
        total[here, :] = sum_here


def residual_far_kernel(far_back, far_ahead, weight, total, out, held, sem):
    load = pltpu.make_async_copy(weight.at[pl.ds(12, 4)], held, sem)
    load.start()
    load.wait()

    @pl.loop(0, 2)
    def _(p):
        here = pl.ds(pl.multiple_of(p * PLEN, PLEN), PLEN)
        sum_here = total[here, :]
        for k in range(SIDE):
            part = (far_back, far_ahead)[k // 2]
            sum_here += jnp.dot(part[k % 2, here, :], held[k], preferred_element_type=jnp.float32)
        out[here, :] = sum_here.astype(jnp.bfloat16)


def scaled(block, gain):
    wide = block.astype(jnp.float32)
    return (wide * gain).astype(jnp.bfloat16), lanes(wide * wide)


def cross_near_kernel(own, back, ahead, weight, gains, total, square):
    @pl.loop(0, 4)
    def _(p):
        here = pl.ds(pl.multiple_of(p * 128, 128), 128)
        for k in range(12):
            part = (own, back, ahead)[k // SIDE]
            block, squares = scaled(part[k % SIDE, here, :], gains[k])
            term = jnp.dot(block, weight[k], preferred_element_type=jnp.float32)
            total[here, :] = term if k == 0 else total[here, :] + term
            square[here, :] = squares if k == 0 else square[here, :] + squares


def cross_far_kernel(far_back, far_ahead, weight, gains, total, square, keys, values, held, sem):
    load = pltpu.make_async_copy(weight.at[pl.ds(12, 4)], held, sem)
    load.start()
    load.wait()

    @pl.loop(0, 4)
    def _(p):
        here = pl.ds(pl.multiple_of(p * 128, 128), 128)
        sum_here, squares = total[here, :], square[here, :]
        for k in range(SIDE):
            part = (far_back, far_ahead)[k // 2]
            block, more = scaled(part[k % 2, here, :], gains[12 + k])
            sum_here += jnp.dot(block, held[k], preferred_element_type=jnp.float32)
            squares += more
        inverse = lax.rsqrt(jnp.sum(squares, axis=1, keepdims=True) / D + epsilon)
        head = (sum_here * inverse).astype(jnp.bfloat16)
        keys[here, :] = head[:, :HD]
        values[here, :] = head[:, HD:]


def bf16(*shape):
    return jax.ShapeDtypeStruct(shape, jnp.bfloat16)


def f32(*shape):
    return jax.ShapeDtypeStruct(shape, jnp.float32)


def call(kernel, outs, ins, scratch, flops, moved, grant=28):
    return pl.pallas_call(
        kernel,
        out_shape=outs,
        in_specs=ins,
        out_specs=jax.tree.map(lambda _: VMEM, outs),
        scratch_shapes=scratch,
        compiler_params=pltpu.CompilerParams(vmem_limit_bytes=grant << 20),
        cost_estimate=pl.CostEstimate(flops=flops, bytes_accessed=moved, transcendentals=0),
    )


def pack_kernel(embedded, attn_gain, final_gain, out):
    tokens = embedded.shape[0]
    out[pl.ds(0, tokens), :] = embedded[...]
    place = lax.broadcasted_iota(jnp.int32, (GAIN_ROWS, HD), 0)
    first = jnp.broadcast_to(attn_gain[...].astype(jnp.float32).reshape(1, HD), (GAIN_ROWS, HD))
    second = jnp.broadcast_to(final_gain[...].astype(jnp.float32).reshape(1, HD), (GAIN_ROWS, HD))
    both = jnp.where(place == 0, first, jnp.where(place == 1, second, 0.0))
    out[pl.ds(tokens, GAIN_ROWS), :] = both.astype(jnp.bfloat16)


def join_kernel(*refs):
    parts, out, sem = refs[:-2], refs[-2], refs[-1]
    copies = [
        pltpu.make_async_copy(part, out.at[:, pl.ds(n * HD, HD)], sem.at[n]) for n, part in enumerate(parts)
    ]
    start_all(copies)
    wait_all(copies)


def side_by_side(*shards):
    return call(
        join_kernel,
        bf16(HD, len(shards) * HD),
        [HBM] * len(shards),
        [pltpu.SemaphoreType.DMA((len(shards),))],
        0,
        len(shards) << 17,
        grant=60,
    )(*shards)


def vmem(*shape, kind=jnp.bfloat16):
    return pltpu.VMEM(shape, kind)


def body(
    token_ids,
    passage_lengths,
    embedding,
    attn_gain,
    final_gain,
    query_weight,
    key_weight,
    value_weight,
    out_weight,
    crosskey_weight,
    crossvalue_weight,
):
    tokens = 2 * PLEN
    dma = pltpu.SemaphoreType.DMA((BLOCKS,))
    place = jnp.stack([lax.axis_index("row"), lax.axis_index("col")]).astype(jnp.int32)
    qkv_weight = side_by_side(query_weight, key_weight, value_weight)
    qkv_other = swap_cores(qkv_weight)
    early = gather_weight(qkv_weight, qkv_other, False)
    embedded = embedding.at[token_ids.reshape(-1)].get(mode="promise_in_bounds")
    chunk = call(
        pack_kernel, bf16(tokens + GAIN_ROWS, HD), [VMEM] * 3, [], 0, 1 << 19
    )(embedded, attn_gain, final_gain)
    parts = gather_direct(chunk)
    rows, square, gains = call(
        prepare_kernel,
        (bf16(tokens, D), f32(tokens, 128), f32(BLOCKS, 1, HD)),
        [SMEM] + [VMEM] * 4,
        [],
        100 * tokens * D * D // 16,
        8 << 20,
    )(place, *parts)
    total = call(
        project_kernel,
        f32(tokens, 3 * HD),
        [VMEM] + [ANY] * 6,
        [vmem(14, HD, 3 * HD), pltpu.SemaphoreType.DMA((6,))],
        2 * tokens * D * 3 * HD,
        10 << 20,
    )(rows, *early[:5], early[6])
    attended = call(
        attend_kernel,
        bf16(tokens, HD),
        [SMEM] + [VMEM] * 5,
        [vmem(3, PLEN, HD)],
        tokens * D * HD,
        4 << 20,
    )(passage_lengths, rows, square, total, early[5], early[7])
    late_weight = side_by_side(out_weight, crosskey_weight, crossvalue_weight)
    late_other = swap_cores(late_weight)
    outer = gather_weight(out_weight, late_other[:, :HD], True)
    cross = gather_weight(late_weight[:, HD:], late_other[:, HD:], True)

    def arrange(weight):
        width = weight[0].shape[1]
        return call(
            arrange_kernel, bf16(BLOCKS, HD, width), [SMEM] + [ANY] * 7, [dma], 0, 4 * D * width
        )(place, *weight)

    parts = gather_halved(attended)
    weight = arrange(outer)
    total = call(
        residual_near_kernel, f32(tokens, HD), [VMEM] * 5, [], 2 * tokens * D * HD, 6 << 20
    )(*parts[:3], weight, embedded)
    hidden = call(
        residual_far_kernel,
        bf16(tokens, HD),
        [VMEM, VMEM, ANY, VMEM],
        [vmem(SIDE, HD, HD), pltpu.SemaphoreType.DMA],
        tokens * D * HD // 2,
        2 << 20,
    )(*parts[3:], weight, total)
    parts = gather_halved(hidden)
    weight = arrange(cross)
    total, square = call(
        cross_near_kernel,
        (f32(tokens, 2 * HD), f32(tokens, 128)),
        [VMEM] * 5,
        [],
        4 * tokens * D * HD,
        8 << 20,
    )(*parts[:3], weight, gains)
    keys, values = call(
        cross_far_kernel,
        (bf16(tokens, HD), bf16(tokens, HD)),
        [VMEM, VMEM, ANY] + [VMEM] * 3,
        [vmem(SIDE, HD, 2 * HD), pltpu.SemaphoreType.DMA],
        tokens * D * HD,
        3 << 20,
    )(*parts[3:], weight, gains, total, square)
    return hidden, keys.reshape(tokens, 1, HD), values.reshape(tokens, 1, HD)


def solution(mesh):
    return jax.shard_map(
        body,
        mesh=mesh,
        in_specs=(
            P("row", None),
            P("row"),
            P(None, "col"),
            P("col"),
            P("col"),
            P("row", "col"),
            P("row", "col"),
            P("row", "col"),
            P("row", "col"),
            P("row", "col"),
            P("row", "col"),
        ),
        out_specs=(P("row", "col"), P("row", "col", None), P("row", "col", None)),
        check_vma=False,
    )
```

profile of v0, /device:TPU:1, one launch (start us, length us, event | category | flops | bytes accessed | tf_op | source)
XLA Modules:
  0.0 164.9 jit_solution(5351828178863169132)
XLA Ops:
  2.5 3.3 %collective-permute-start.6 = (bf16[256,768]{1,0:T(8,128)(2,1)}, bf16[256,768]{1,0:T(8,128)(2,1)S(1)}, u32[]{:S(2)}, u32[]{:S(2)}) collective-permute-start(bf16[256,768]{1,0:T(8,128)(2,1)} %shard_map.132.own), channel_id=1, source_target_pairs={{0,16},{1,17},{2,18},{3,19},{4,20},{5,21},{6,22},{7,23},{8,24},{9,... | collective-permute-start | bytes 1179656 | tf_op jit(solution)/shard_map/ppermute | solution.py:43
  8.6 3.9 %collective-permute-start.7 = (bf16[2,256,768]{2,1,0:T(8,128)(2,1)S(1)}, bf16[2,256,768]{2,1,0:T(8,128)(2,1)S(1)}, u32[]{:S(2)}, u32[]{:S(2)}) collective-permute-start(bf16[2,256,768]{2,1,0:T(8,128)(2,1)S(1)} %pad_maximum_fusion.6), channel_id=1, source_target_pairs={{0,32},{1,33},{2,34},{3,35},{4,36},{5,37},{6,38},{7,39},{8,40},{9,... | collective-permute-start | bytes 2359304 | tf_op jit(solution)/shard_map/ppermute | solution.py:43
  12.5 8.9 %collective-permute-done.7.hop1 = bf16[2,256,768]{2,1,0:T(8,128)(2,1)S(1)} collective-permute-done((bf16[2,256,768]{2,1,0:T(8,128)(2,1)S(1)}, bf16[2,256,768]{2,1,0:T(8,128)(2,1)S(1)}, u32[]{:S(2)}, u32[]{:S(2)}) %collective-permute-start.7) | collective-permute-done | bytes 786464 | tf_op jit(solution)/shard_map/ppermute | solution.py:43
  21.4 3.1 %collective-permute-start.8 = (bf16[2,256,768]{2,1,0:T(8,128)(2,1)S(1)}, bf16[2,256,768]{2,1,0:T(8,128)(2,1)}, u32[]{:S(2)}, u32[]{:S(2)}) collective-permute-start(bf16[2,256,768]{2,1,0:T(8,128)(2,1)S(1)} %collective-permute-done.7.hop1), channel_id=1, source_target_pairs={{0,32},{1,33},{2,34},{3,35},{4,36},{5,37},{6,38},{7,39},{8,40},{9,... | collective-permute-start | bytes 2359304 | tf_op jit(solution)/shard_map/ppermute | solution.py:43
  24.6 6.0 %gather_fusion = bf16[512,256]{1,0:T(8,128)(2,1)S(1)} fusion(bf16[16384,256]{1,0:T(8,128)(2,1)} %param.13, s32[1024]{0:T(1024)S(1)} %pad_clamp_fusion), kind=kCustom, calls=%fused_computation | custom fusion | bytes 526336 | tf_op jit(solution)/shard_map/gather | solution.py:376
  49.6 3.4 %collective-permute-start.33 = (bf16[2,256,512]{2,1,0:T(8,128)(2,1)}, bf16[2,256,512]{2,1,0:T(8,128)(2,1)S(1)}, u32[]{:S(2)}, u32[]{:S(2)}) collective-permute-start(bf16[2,256,512]{2,1,0:T(8,128)(2,1)} %pad_maximum_fusion.7), channel_id=1, source_target_pairs={{0,32},{1,33},{2,34},{3,35},{4,36},{5,37},{6,38},{7,39},{8,40},{9,... | collective-permute-start | bytes 1572872 | tf_op jit(solution)/shard_map/ppermute | solution.py:43
  59.4 3.0 %collective-permute-start.22 = (bf16[2,256,256]{2,1,0:T(8,128)(2,1)}, bf16[2,256,256]{2,1,0:T(8,128)(2,1)S(1)}, u32[]{:S(2)}, u32[]{:S(2)}) collective-permute-start(bf16[2,256,256]{2,1,0:T(8,128)(2,1)} %collective-permute-done.21.refs_3_), channel_id=1, source_target_pairs={{0,32},{1,33},{2,34},{3,35},{4,36},{5,37},{6,38},{7,39},{8,40},{9,... | collective-permute-start | bytes 786440 | tf_op jit(solution)/shard_map/ppermute | solution.py:43
  62.5 2.3 %collective-permute-start.10 = (bf16[6,256,768]{2,1,0:T(8,128)(2,1)S(1)}, bf16[6,256,768]{2,1,0:T(8,128)(2,1)S(1)}, u32[]{:S(2)}, u32[]{:S(2)}) collective-permute-start(bf16[6,256,768]{2,1,0:T(8,128)(2,1)S(1)} %pad_maximum_fusion), channel_id=1, source_target_pairs={{0,16},{1,17},{2,18},{3,19},{4,20},{5,21},{6,22},{7,23},{8,24},{9,... | collective-permute-start | bytes 7077896 | tf_op jit(solution)/shard_map/ppermute | solution.py:43
  67.0 4.6 %collective-permute-done.5.far = bf16[4,528,256]{2,1,0:T(8,128)(2,1)} collective-permute-done((bf16[4,528,256]{2,1,0:T(8,128)(2,1)S(1)}, bf16[4,528,256]{2,1,0:T(8,128)(2,1)}, u32[]{:S(2)}, u32[]{:S(2)}) %collective-permute-start.5) | collective-permute-done | bytes 1081376 | tf_op jit(solution)/shard_map/ppermute | solution.py:43
  71.5 3.9 %shard_map.131 = (bf16[512,4096]{1,0:T(8,128)(2,1)S(1)}, f32[512,128]{1,0:T(8,128)S(1)}, f32[16,1,256]{2,1,0:T(1,128)S(1)}) custom-call(s32[2]{0:T(128)S(1)} %pad_add_fusion.place_ref.refs_0_, bf16[4,528,256]{2,1,0:T(8,128)(2,1)S(1)} %pad_maximum_fusion.2.own, bf16[4,528,256]{2,1,0:T(8,128)(2,1)} %collective-permute-done.3.back, ...), custom_call_target="tpu_custom_call" | custom-call | flops 53687091200 | bytes 8388608 | tf_op jit(solution)/shard_map/pallas_call | solution.py:381
  75.5 5.6 %shard_map.133.total = f32[512,768]{1,0:T(8,128)S(1)} custom-call(bf16[512,4096]{1,0:T(8,128)(2,1)S(1)} %get-tuple-element.10.rows, bf16[256,768]{1,0:T(8,128)(2,1)S(1)} %copy-done, bf16[256,768]{1,0:T(8,128)(2,1)S(1)} %copy-done.5, bf16[2,256,768]{2,1,0:T(8,128)(2,1)S(1)} %copy-done.3, bf16[2,256,768]{2,1,0:T(8,128)(2,1)} %collective-permute-done.8.hop2, ...), custom_call_target="tpu_custom_call" | custom-call | flops 3221225472 | bytes 10485760 | tf_op jit(solution)/shard_map/pallas_call | solution.py:389
  81.1 2.7 %shard_map.134 = bf16[512,256]{1,0:T(8,128)(2,1)S(1)} custom-call(s32[2]{0:T(128)S(1)} %copy-done.6, bf16[512,4096]{1,0:T(8,128)(2,1)S(1)} %get-tuple-element.10.rows, f32[512,128]{1,0:T(8,128)S(1)} %get-tuple-element.11.square, f32[512,768]{1,0:T(8,128)S(1)} %shard_map.133.total, bf16[256,768]{1,0:T(8,128)(2,1)} %collective-permute-done.11.far, ...), custom_call_target="tpu_custom_call" | custom-call | flops 536870912 | bytes 4194304 | tf_op jit(solution)/shard_map/pallas_call | solution.py:397
  84.4 2.3 %collective-permute-start.14 = (bf16[512,256]{1,0:T(8,128)(2,1)S(1)}, bf16[512,256]{1,0:T(8,128)(2,1)S(1)}, u32[]{:S(2)}, u32[]{:S(2)}) collective-permute-start(bf16[512,256]{1,0:T(8,128)(2,1)S(1)} %shard_map.134), channel_id=1, source_target_pairs={{0,12},{1,13},{2,14},{3,15},{4,0},{5,1},{6,2},{7,3},{8,4},{9,5},{1... | collective-permute-start | bytes 786440 | tf_op jit(solution)/shard_map/ppermute | solution.py:43
  87.8 2.7 %collective-permute-start.23 = (bf16[2,256,256]{2,1,0:T(8,128)(2,1)S(1)}, bf16[2,256,256]{2,1,0:T(8,128)(2,1)S(1)}, u32[]{:S(2)}, u32[]{:S(2)}) collective-permute-start(bf16[2,256,256]{2,1,0:T(8,128)(2,1)S(1)} %collective-permute-done.22.refs_4_), channel_id=1, source_target_pairs={{0,32},{1,33},{2,34},{3,35},{4,36},{5,37},{6,38},{7,39},{8,40},{9,... | collective-permute-start | bytes 786440 | tf_op jit(solution)/shard_map/ppermute | solution.py:43
  97.5 2.7 %collective-permute-start.35 = (bf16[2,256,512]{2,1,0:T(8,128)(2,1)S(1)}, bf16[2,256,512]{2,1,0:T(8,128)(2,1)S(1)}, u32[]{:S(2)}, u32[]{:S(2)}) collective-permute-start(bf16[2,256,512]{2,1,0:T(8,128)(2,1)S(1)} %collective-permute-done.34.refs_4_), channel_id=1, source_target_pairs={{0,32},{1,33},{2,34},{3,35},{4,36},{5,37},{6,38},{7,39},{8,40},{9,... | collective-permute-start | bytes 1572872 | tf_op jit(solution)/shard_map/ppermute | solution.py:43
  100.9 6.9 %collective-permute-done.24.refs_6_ = bf16[256,256]{1,0:T(8,128)(2,1)S(1)} collective-permute-done((bf16[256,256]{1,0:T(8,128)(2,1)S(1)}, bf16[256,256]{1,0:T(8,128)(2,1)S(1)}, u32[]{:S(2)}, u32[]{:S(2)}) %collective-permute-start.24) | collective-permute-done | bytes 131104 | tf_op jit(solution)/shard_map/ppermute | solution.py:43
  108.8 3.3 %collective-permute-start.25 = (bf16[7,256,256]{2,1,0:T(8,128)(2,1)S(1)}, bf16[7,256,256]{2,1,0:T(8,128)(2,1)S(1)}, u32[]{:S(2)}, u32[]{:S(2)}) collective-permute-start(bf16[7,256,256]{2,1,0:T(8,128)(2,1)S(1)} %pad_maximum_fusion.5), channel_id=1, source_target_pairs={{0,16},{1,17},{2,18},{3,19},{4,20},{5,21},{6,22},{7,23},{8,24},{9,... | collective-permute-start | bytes 2752520 | tf_op jit(solution)/shard_map/ppermute | solution.py:43
  120.2 3.8 %shard_map.136.weight = bf16[16,256,256]{2,1,0:T(8,128)(2,1)S(1)} custom-call(s32[2]{0:T(128)S(1)} %pad_add_fusion.place_ref.refs_0_, bf16[256,256]{1,0:T(8,128)(2,1)S(1)} %copy-done.1, bf16[256,256]{1,0:T(8,128)(2,1)S(1)} %get-tuple-element.22.refs_2_, bf16[2,256,256]{2,1,0:T(8,128)(2,1)} %collective-permute-done.21.refs_3_, ...), custom_call_target="tpu_custom_call" | custom-call | bytes 4194304 | tf_op jit(solution)/shard_map/pallas_call | solution.py:412
  126.7 2.7 %collective-permute-start.27 = (bf16[512,256]{1,0:T(8,128)(2,1)}, bf16[512,256]{1,0:T(8,128)(2,1)S(1)}, u32[]{:S(2)}, u32[]{:S(2)}) collective-permute-start(bf16[512,256]{1,0:T(8,128)(2,1)} %shard_map.138), channel_id=1, source_target_pairs={{0,12},{1,13},{2,14},{3,15},{4,0},{5,1},{6,2},{7,3},{8,4},{9,5},{1... | collective-permute-start | bytes 786440 | tf_op jit(solution)/shard_map/ppermute | solution.py:43
  129.3 4.3 %collective-permute-done.26 = bf16[512,256]{1,0:T(8,128)(2,1)S(1)} collective-permute-done((bf16[512,256]{1,0:T(8,128)(2,1)}, bf16[512,256]{1,0:T(8,128)(2,1)S(1)}, u32[]{:S(2)}, u32[]{:S(2)}) %collective-permute-start.26) | collective-permute-done | bytes 262176 | tf_op jit(solution)/shard_map/ppermute | solution.py:43
  140.4 12.5 %collective-permute-done.29.back = bf16[4,512,256]{2,1,0:T(8,128)(2,1)S(1)} collective-permute-done((bf16[4,512,256]{2,1,0:T(8,128)(2,1)S(1)}, bf16[4,512,256]{2,1,0:T(8,128)(2,1)S(1)}, u32[]{:S(2)}, u32[]{:S(2)}) %collective-permute-start.29) | collective-permute-done | bytes 1048608 | tf_op jit(solution)/shard_map/ppermute | solution.py:43
  153.1 2.7 %collective-permute-start.32 = (bf16[2,512,256]{2,1,0:T(8,128)(2,1)S(1)}, bf16[2,512,256]{2,1,0:T(8,128)(2,1)S(1)}, u32[]{:S(2)}, u32[]{:S(2)}) collective-permute-start(bf16[2,512,256]{2,1,0:T(8,128)(2,1)S(1)} %slice.48), channel_id=1, source_target_pairs={{0,3},{1,0},{2,1},{3,2},{4,7},{5,4},{6,5},{7,6},{8,11},{9,8},{10,9... | collective-permute-start | bytes 1572872 | tf_op jit(solution)/shard_map/ppermute | solution.py:43
  157.1 2.5 %shard_map.140 = (f32[512,512]{1,0:T(8,128)S(1)}, f32[512,128]{1,0:T(8,128)S(1)}) custom-call(bf16[4,512,256]{2,1,0:T(8,128)(2,1)S(1)} %pad_maximum_fusion.4.own, bf16[4,512,256]{2,1,0:T(8,128)(2,1)S(1)} %collective-permute-done.29.back, bf16[4,512,256]{2,1,0:T(8,128)(2,1)S(1)} %collective-permute-done.31.ahead, ...), custom_call_target="tpu_custom_call" | custom-call | flops 2147483648 | bytes 8388608 | tf_op jit(solution)/shard_map/pallas_call | solution.py:431
  159.6 2.9 %collective-permute-done.30.far_back = bf16[2,512,256]{2,1,0:T(8,128)(2,1)S(1)} collective-permute-done((bf16[2,512,256]{2,1,0:T(8,128)(2,1)S(1)}, bf16[2,512,256]{2,1,0:T(8,128)(2,1)S(1)}, u32[]{:S(2)}, u32[]{:S(2)}) %collective-permute-start.30) | collective-permute-done | bytes 524320 | tf_op jit(solution)/shard_map/ppermute | solution.py:43
  (112 shorter events, 63.7 us)
Async XLA Ops:
  8.6 12.9 %collective-permute-start.7 = (bf16[2,256,768]{2,1,0:T(8,128)(2,1)S(1)}, bf16[2,256,768]{2,1,0:T(8,128)(2,1)S(1)}, u32[]{:S(2)}, u32[]{:S(2)}) collective-permute-start(bf16[2,256,768]{2,1,0:T(8,128)(2,1)S(1)} %pad_maximum_fusion.6), channel_id=1, source_target_pairs={{0,32},{1,33},{2,34},{3,35},{4,36},{5,37},{6,38},{7,39},{8,40},{9,... | collective-permute-start | bytes 2359304 | tf_op jit(solution)/shard_map/ppermute | solution.py:43
  21.4 16.6 %collective-permute-start.8 = (bf16[2,256,768]{2,1,0:T(8,128)(2,1)S(1)}, bf16[2,256,768]{2,1,0:T(8,128)(2,1)}, u32[]{:S(2)}, u32[]{:S(2)}) collective-permute-start(bf16[2,256,768]{2,1,0:T(8,128)(2,1)S(1)} %collective-permute-done.7.hop1), channel_id=1, source_target_pairs={{0,32},{1,33},{2,34},{3,35},{4,36},{5,37},{6,38},{7,39},{8,40},{9,... | collective-permute-start | bytes 2359304 | tf_op jit(solution)/shard_map/ppermute | solution.py:43
  30.7 9.7 %collective-permute-start = (bf16[528,256]{1,0:T(8,128)(2,1)S(1)}, bf16[528,256]{1,0:T(8,128)(2,1)S(1)}, u32[]{:S(2)}, u32[]{:S(2)}) collective-permute-start(bf16[528,256]{1,0:T(8,128)(2,1)S(1)} %shard_map.130), channel_id=1, source_target_pairs={{0,4},{1,5},{2,6},{3,7},{4,8},{5,9},{6,10},{7,11},{8,12},{9,13},{1... | collective-permute-start | bytes 811016 | tf_op jit(solution)/shard_map/ppermute | solution.py:43
  37.0 10.6 %collective-permute-start.20 = (bf16[256,768]{1,0:T(8,128)(2,1)}, bf16[256,768]{1,0:T(8,128)(2,1)S(1)}, u32[]{:S(2)}, u32[]{:S(2)}) collective-permute-start(bf16[256,768]{1,0:T(8,128)(2,1)} %shard_map.135), channel_id=1, source_target_pairs={{0,16},{1,17},{2,18},{3,19},{4,20},{5,21},{6,22},{7,23},{8,24},{9,... | collective-permute-start | bytes 1179656 | tf_op jit(solution)/shard_map/ppermute | solution.py:43
  38.1 11.5 %collective-permute-start.9 = (bf16[2,256,768]{2,1,0:T(8,128)(2,1)}, bf16[2,256,768]{2,1,0:T(8,128)(2,1)S(1)}, u32[]{:S(2)}, u32[]{:S(2)}) collective-permute-start(bf16[2,256,768]{2,1,0:T(8,128)(2,1)} %collective-permute-done.8.hop2), channel_id=1, source_target_pairs={{0,32},{1,33},{2,34},{3,35},{4,36},{5,37},{6,38},{7,39},{8,40},{9,... | collective-permute-start | bytes 2359304 | tf_op jit(solution)/shard_map/ppermute | solution.py:43
  43.3 19.2 %collective-permute-start.3 = (bf16[4,528,256]{2,1,0:T(8,128)(2,1)S(1)}, bf16[4,528,256]{2,1,0:T(8,128)(2,1)}, u32[]{:S(2)}, u32[]{:S(2)}) collective-permute-start(bf16[4,528,256]{2,1,0:T(8,128)(2,1)S(1)} %pad_maximum_fusion.2.own), channel_id=1, source_target_pairs={{0,1},{1,2},{2,3},{3,0},{4,5},{5,6},{6,7},{7,4},{8,9},{9,10},{10,1... | collective-permute-start | bytes 3244040 | tf_op jit(solution)/shard_map/ppermute | solution.py:43
  44.6 17.9 %collective-permute-start.4 = (bf16[4,528,256]{2,1,0:T(8,128)(2,1)S(1)}, bf16[4,528,256]{2,1,0:T(8,128)(2,1)}, u32[]{:S(2)}, u32[]{:S(2)}) collective-permute-start(bf16[4,528,256]{2,1,0:T(8,128)(2,1)S(1)} %pad_maximum_fusion.2.own), channel_id=1, source_target_pairs={{0,3},{1,0},{2,1},{3,2},{4,7},{5,4},{6,5},{7,6},{8,11},{9,8},{10,9... | collective-permute-start | bytes 3244040 | tf_op jit(solution)/shard_map/ppermute | solution.py:43
  46.0 25.5 %collective-permute-start.5 = (bf16[4,528,256]{2,1,0:T(8,128)(2,1)S(1)}, bf16[4,528,256]{2,1,0:T(8,128)(2,1)}, u32[]{:S(2)}, u32[]{:S(2)}) collective-permute-start(bf16[4,528,256]{2,1,0:T(8,128)(2,1)S(1)} %pad_maximum_fusion.2.own), channel_id=1, source_target_pairs={{0,2},{1,3},{2,0},{3,1},{4,6},{5,7},{6,4},{7,5},{8,10},{9,11},{10,... | collective-permute-start | bytes 3244040 | tf_op jit(solution)/shard_map/ppermute | solution.py:43
  49.6 9.8 %collective-permute-start.33 = (bf16[2,256,512]{2,1,0:T(8,128)(2,1)}, bf16[2,256,512]{2,1,0:T(8,128)(2,1)S(1)}, u32[]{:S(2)}, u32[]{:S(2)}) collective-permute-start(bf16[2,256,512]{2,1,0:T(8,128)(2,1)} %pad_maximum_fusion.7), channel_id=1, source_target_pairs={{0,32},{1,33},{2,34},{3,35},{4,36},{5,37},{6,38},{7,39},{8,40},{9,... | collective-permute-start | bytes 1572872 | tf_op jit(solution)/shard_map/ppermute | solution.py:43
  53.8 11.0 %collective-permute-start.11 = (bf16[256,768]{1,0:T(8,128)(2,1)}, bf16[256,768]{1,0:T(8,128)(2,1)}, u32[]{:S(2)}, u32[]{:S(2)}) collective-permute-start(bf16[256,768]{1,0:T(8,128)(2,1)} %slice_bitcast_fusion), channel_id=1, source_target_pairs={{0,32},{1,33},{2,34},{3,35},{4,36},{5,37},{6,38},{7,39},{8,40},{9,... | collective-permute-start | bytes 1179656 | tf_op jit(solution)/shard_map/ppermute | solution.py:43
  59.4 28.4 %collective-permute-start.22 = (bf16[2,256,256]{2,1,0:T(8,128)(2,1)}, bf16[2,256,256]{2,1,0:T(8,128)(2,1)S(1)}, u32[]{:S(2)}, u32[]{:S(2)}) collective-permute-start(bf16[2,256,256]{2,1,0:T(8,128)(2,1)} %collective-permute-done.21.refs_3_), channel_id=1, source_target_pairs={{0,32},{1,33},{2,34},{3,35},{4,36},{5,37},{6,38},{7,39},{8,40},{9,... | collective-permute-start | bytes 786440 | tf_op jit(solution)/shard_map/ppermute | solution.py:43
  62.4 35.1 %collective-permute-start.34 = (bf16[2,256,512]{2,1,0:T(8,128)(2,1)S(1)}, bf16[2,256,512]{2,1,0:T(8,128)(2,1)S(1)}, u32[]{:S(2)}, u32[]{:S(2)}) collective-permute-start(bf16[2,256,512]{2,1,0:T(8,128)(2,1)S(1)} %collective-permute-done.33.refs_3_), channel_id=1, source_target_pairs={{0,32},{1,33},{2,34},{3,35},{4,36},{5,37},{6,38},{7,39},{8,40},{9,... | collective-permute-start | bytes 1572872 | tf_op jit(solution)/shard_map/ppermute | solution.py:43
  62.5 13.0 %collective-permute-start.10 = (bf16[6,256,768]{2,1,0:T(8,128)(2,1)S(1)}, bf16[6,256,768]{2,1,0:T(8,128)(2,1)S(1)}, u32[]{:S(2)}, u32[]{:S(2)}) collective-permute-start(bf16[6,256,768]{2,1,0:T(8,128)(2,1)S(1)} %pad_maximum_fusion), channel_id=1, source_target_pairs={{0,16},{1,17},{2,18},{3,19},{4,20},{5,21},{6,22},{7,23},{8,24},{9,... | collective-permute-start | bytes 7077896 | tf_op jit(solution)/shard_map/ppermute | solution.py:43
  64.7 16.3 %collective-permute-start.12 = (bf16[256,768]{1,0:T(8,128)(2,1)}, bf16[256,768]{1,0:T(8,128)(2,1)S(1)}, u32[]{:S(2)}, u32[]{:S(2)}) collective-permute-start(bf16[256,768]{1,0:T(8,128)(2,1)} %collective-permute-done.11.far), channel_id=1, source_target_pairs={{0,16},{1,17},{2,18},{3,19},{4,20},{5,21},{6,22},{7,23},{8,24},{9,... | collective-permute-start | bytes 1179656 | tf_op jit(solution)/shard_map/ppermute | solution.py:43
  87.8 12.4 %collective-permute-start.23 = (bf16[2,256,256]{2,1,0:T(8,128)(2,1)S(1)}, bf16[2,256,256]{2,1,0:T(8,128)(2,1)S(1)}, u32[]{:S(2)}, u32[]{:S(2)}) collective-permute-start(bf16[2,256,256]{2,1,0:T(8,128)(2,1)S(1)} %collective-permute-done.22.refs_4_), channel_id=1, source_target_pairs={{0,32},{1,33},{2,34},{3,35},{4,36},{5,37},{6,38},{7,39},{8,40},{9,... | collective-permute-start | bytes 786440 | tf_op jit(solution)/shard_map/ppermute | solution.py:43
  94.8 19.0 %collective-permute-start.16 = (bf16[4,512,256]{2,1,0:T(8,128)(2,1)S(1)}, bf16[4,512,256]{2,1,0:T(8,128)(2,1)S(1)}, u32[]{:S(2)}, u32[]{:S(2)}) collective-permute-start(bf16[4,512,256]{2,1,0:T(8,128)(2,1)S(1)} %pad_maximum_fusion.3.own), channel_id=1, source_target_pairs={{0,1},{1,2},{2,3},{3,0},{4,5},{5,6},{6,7},{7,4},{8,9},{9,10},{10,1... | collective-permute-start | bytes 3145736 | tf_op jit(solution)/shard_map/ppermute | solution.py:43
  95.7 19.4 %collective-permute-start.18 = (bf16[4,512,256]{2,1,0:T(8,128)(2,1)S(1)}, bf16[4,512,256]{2,1,0:T(8,128)(2,1)S(1)}, u32[]{:S(2)}, u32[]{:S(2)}) collective-permute-start(bf16[4,512,256]{2,1,0:T(8,128)(2,1)S(1)} %pad_maximum_fusion.3.own), channel_id=1, source_target_pairs={{0,3},{1,0},{2,1},{3,2},{4,7},{5,4},{6,5},{7,6},{8,11},{9,8},{10,9... | collective-permute-start | bytes 3145736 | tf_op jit(solution)/shard_map/ppermute | solution.py:43
  97.5 14.6 %collective-permute-start.35 = (bf16[2,256,512]{2,1,0:T(8,128)(2,1)S(1)}, bf16[2,256,512]{2,1,0:T(8,128)(2,1)S(1)}, u32[]{:S(2)}, u32[]{:S(2)}) collective-permute-start(bf16[2,256,512]{2,1,0:T(8,128)(2,1)S(1)} %collective-permute-done.34.refs_4_), channel_id=1, source_target_pairs={{0,32},{1,33},{2,34},{3,35},{4,36},{5,37},{6,38},{7,39},{8,40},{9,... | collective-permute-start | bytes 1572872 | tf_op jit(solution)/shard_map/ppermute | solution.py:43
  108.8 11.4 %collective-permute-start.25 = (bf16[7,256,256]{2,1,0:T(8,128)(2,1)S(1)}, bf16[7,256,256]{2,1,0:T(8,128)(2,1)S(1)}, u32[]{:S(2)}, u32[]{:S(2)}) collective-permute-start(bf16[7,256,256]{2,1,0:T(8,128)(2,1)S(1)} %pad_maximum_fusion.5), channel_id=1, source_target_pairs={{0,16},{1,17},{2,18},{3,19},{4,20},{5,21},{6,22},{7,23},{8,24},{9,... | collective-permute-start | bytes 2752520 | tf_op jit(solution)/shard_map/ppermute | solution.py:43
  113.8 11.4 %collective-permute-start.17 = (bf16[2,512,256]{2,1,0:T(8,128)(2,1)S(1)}, bf16[2,512,256]{2,1,0:T(8,128)(2,1)S(1)}, u32[]{:S(2)}, u32[]{:S(2)}) collective-permute-start(bf16[2,512,256]{2,1,0:T(8,128)(2,1)S(1)} %slice.43), channel_id=1, source_target_pairs={{0,1},{1,2},{2,3},{3,0},{4,5},{5,6},{6,7},{7,4},{8,9},{9,10},{10,1... | collective-permute-start | bytes 1572872 | tf_op jit(solution)/shard_map/ppermute | solution.py:43
  115.1 10.1 %collective-permute-start.19 = (bf16[2,512,256]{2,1,0:T(8,128)(2,1)S(1)}, bf16[2,512,256]{2,1,0:T(8,128)(2,1)S(1)}, u32[]{:S(2)}, u32[]{:S(2)}) collective-permute-start(bf16[2,512,256]{2,1,0:T(8,128)(2,1)S(1)} %slice.44), channel_id=1, source_target_pairs={{0,3},{1,0},{2,1},{3,2},{4,7},{5,4},{6,5},{7,6},{8,11},{9,8},{10,9... | collective-permute-start | bytes 1572872 | tf_op jit(solution)/shard_map/ppermute | solution.py:43
  118.0 37.8 %collective-permute-start.37 = (bf16[7,256,512]{2,1,0:T(8,128)(2,1)S(1)}, bf16[7,256,512]{2,1,0:T(8,128)(2,1)S(1)}, u32[]{:S(2)}, u32[]{:S(2)}) collective-permute-start(bf16[7,256,512]{2,1,0:T(8,128)(2,1)S(1)} %pad_maximum_fusion.1), channel_id=1, source_target_pairs={{0,16},{1,17},{2,18},{3,19},{4,20},{5,21},{6,22},{7,23},{8,24},{9,... | collective-permute-start | bytes 5505032 | tf_op jit(solution)/shard_map/ppermute | solution.py:43
  137.7 15.2 %collective-permute-start.29 = (bf16[4,512,256]{2,1,0:T(8,128)(2,1)S(1)}, bf16[4,512,256]{2,1,0:T(8,128)(2,1)S(1)}, u32[]{:S(2)}, u32[]{:S(2)}) collective-permute-start(bf16[4,512,256]{2,1,0:T(8,128)(2,1)S(1)} %pad_maximum_fusion.4.own), channel_id=1, source_target_pairs={{0,1},{1,2},{2,3},{3,0},{4,5},{5,6},{6,7},{7,4},{8,9},{9,10},{10,1... | collective-permute-start | bytes 3145736 | tf_op jit(solution)/shard_map/ppermute | solution.py:43
  138.4 14.6 %collective-permute-start.31 = (bf16[4,512,256]{2,1,0:T(8,128)(2,1)S(1)}, bf16[4,512,256]{2,1,0:T(8,128)(2,1)S(1)}, u32[]{:S(2)}, u32[]{:S(2)}) collective-permute-start(bf16[4,512,256]{2,1,0:T(8,128)(2,1)S(1)} %pad_maximum_fusion.4.own), channel_id=1, source_target_pairs={{0,3},{1,0},{2,1},{3,2},{4,7},{5,4},{6,5},{7,6},{8,11},{9,8},{10,9... | collective-permute-start | bytes 3145736 | tf_op jit(solution)/shard_map/ppermute | solution.py:43
  (26 other events, 281.1 us)
where the time goes:
time: 167 us; the launch traced here: 165 us
  starting transfers between devices  66 us (40%)
  waiting for transfers between devices  53.4 us (32%)
  Pallas kernels  28 us (17%)
  local copies, waits for them, and re-layouts  8.74 us (5%)
  other arithmetic  7.53 us (5%)
    ppermute x38, starting transfers between devices, send(): return lax.ppermute(block, ('row', 'col'), moves(step))  66 us
    ppermute x38, waiting for transfers between devices, send(): return lax.ppermute(block, ('row', 'col'), moves(step))  53.4 us
    gather x1, local copies, waits for them, and re-layouts, body(): embedded = embedding.at[token_ids.reshape(-1)].get(mode='promise_in_bounds')  6.02 us
    pallas_call x1, Pallas kernels, body(): call(project_kernel, f32(tokens, 3 * HD), [VMEM] + [ANY] * 6, [vmem(14, H...  5.56 us
    pallas_call x2, Pallas kernels, arrange(): call(arrange_kernel, bf16(BLOCKS, HD, width), [SMEM] + [ANY] * 7, [dma],...  5.08 us
    pallas_call x1, Pallas kernels, body(): call(prepare_kernel, (bf16(tokens, D), f32(tokens, 128), f32(BLOCKS, 1, H...  3.88 us
    pallas_call x2, Pallas kernels, side_by_side(): call(join_kernel, bf16(HD, len(shards) * HD), [HBM] * len(shards), [pltpu...  3.61 us
  transfers between devices with their start and end apart: 38, of which 16 were waited for; matrix products, arithmetic and copies ran while one was open for 9% of the time, Pallas kernels for 15%

commit v1 on v0

--- a/solution.py
+++ b/solution.py
@@ -68,10 +68,13 @@
     return [stack] + [second_leg(stack, s) for s in SHIFTS]
 
 
-def gather_halved(chunk):
-    stack = gather_first(chunk)
-    back, ahead = second_leg(stack, 1), second_leg(stack, 3)
-    return [stack, back, ahead, second_leg(back[:2], 1), second_leg(ahead[2:], 3)]
+def gather_split(chunk):
+    back, ahead, far = (first_leg(chunk, s) for s in SHIFTS)
+    low, high = jnp.stack([chunk, back]), jnp.stack([ahead, far])
+    back_low, ahead_high = second_leg(low, 1), second_leg(high, 3)
+    back_high, ahead_low = second_leg(high, 1), second_leg(low, 3)
+    passed = [second_leg(back_low, 1), second_leg(ahead_high, 3)]
+    return [low, high, back_low, back_high, ahead_low, ahead_high], passed
 
 
 def gather_weight(shard, other, late):
@@ -131,8 +134,9 @@
 
 def block_of(place, first, second):
     c = place[1]
-    x = place[2] + OFFSETS[first] * (1 - c) + OFFSETS[second] * c
-    y = place[3] + OFFSETS[first] * c + OFFSETS[second] * (1 - c)
+    away = jnp.where(first == 0, 0, jnp.where(first == 1, 3, first - 1))
+    x = place[2] + away * (1 - c) + OFFSETS[second] * c
+    y = place[3] + away * c + OFFSETS[second] * (1 - c)
     return lax.rem(x, SIDE) * SIDE + lax.rem(y, SIDE)
 
 
@@ -158,8 +162,11 @@
 def prepare_kernel(place_ref, own, back, ahead, far, rows, square, final_ref):
     place = read(place_ref)
     tokens, step = rows.shape[0], 64
+    square[...] = jnp.zeros_like(square)
     for second, part in enumerate((own, back, ahead, far)):
-        for first in range(SIDE):
+
+        @pl.loop(0, SIDE)
+        def _(first):
             spot = arrival(place, block_of(place, first, second))
             there = pl.ds(pl.multiple_of(spot * HD, HD), HD)
             gains = part[first, pl.ds(tokens, GAIN_ROWS), :].astype(jnp.float32)
@@ -170,8 +177,7 @@
             def _(tile):
                 here = pl.ds(pl.multiple_of(tile * step, step), step)
                 wide = part[first, here, :].astype(jnp.float32)
-                total = lanes(wide * wide)
-                square[here, :] = total if second + first == 0 else square[here, :] + total
+                square[here, :] += lanes(wide * wide)
                 rows[here, there] = (wide * gain).astype(jnp.bfloat16)
 
 
@@ -194,10 +200,10 @@
     wait_all(copies)
     weight = held.reshape(14 * HD, 3 * HD)
 
-    @pl.loop(0, 6)
+    @pl.loop(0, 12)
     def _(n):
-        here = pl.ds(pl.multiple_of(lax.div(n, 3) * PLEN, PLEN), PLEN)
-        there = pl.ds(pl.multiple_of(lax.rem(n, 3) * HD, HD), HD)
+        here = pl.ds(pl.multiple_of(lax.rem(n, 4) * 128, 128), 128)
+        there = pl.ds(pl.multiple_of(lax.div(n, 4) * HD, HD), HD)
         total[here, there] = jnp.dot(
             rows[here, : 14 * HD], weight[:, there], preferred_element_type=jnp.float32
         )
@@ -209,12 +215,15 @@
         here = pl.ds(pl.multiple_of(p * PLEN, PLEN), PLEN)
         mean = jnp.sum(square[here, :], axis=1, keepdims=True) / D
         inverse = lax.rsqrt(mean + epsilon)
-        for n in range(3):
-            there = pl.ds(n * HD, HD)
+
+        @pl.loop(0, 3)
+        def _(n):
+            there = pl.ds(pl.multiple_of(n * HD, HD), HD)
             head = total[here, there]
             head += jnp.dot(rows[here, 14 * HD : 15 * HD], far[:, there], preferred_element_type=jnp.float32)
             head += jnp.dot(rows[here, 15 * HD :], far_crossed[:, there], preferred_element_type=jnp.float32)
             heads[n] = (head * inverse).astype(jnp.bfloat16)
+
         scores = lax.dot_general(
             heads[0], heads[1], (((1,), (1,)), ((), ())), preferred_element_type=jnp.float32
         ) * HD ** (-0.5)
@@ -236,14 +245,15 @@
     wait_all(copies)
 
 
-def residual_near_kernel(own, back, ahead, weight, embedded, total):
-    @pl.loop(0, 2)
+def residual_near_kernel(*refs):
+    parts, (weight, embedded, total) = refs[:6], refs[6:]
+
+    @pl.loop(0, 4)
     def _(p):
-        here = pl.ds(pl.multiple_of(p * PLEN, PLEN), PLEN)
+        here = pl.ds(pl.multiple_of(p * 128, 128), 128)
         sum_here = embedded[here, :].astype(jnp.float32)
         for k in range(12):
-            part = (own, back, ahead)[k // SIDE]
-            sum_here += jnp.dot(part[k % SIDE, here, :], weight[k], preferred_element_type=jnp.float32)
+            sum_here += jnp.dot(parts[k // 2][k % 2, here, :], weight[k], preferred_element_type=jnp.float32)
         total[here, :] = sum_here
 
 
@@ -252,9 +262,9 @@
     load.start()
     load.wait()
 
-    @pl.loop(0, 2)
+    @pl.loop(0, 4)
     def _(p):
-        here = pl.ds(pl.multiple_of(p * PLEN, PLEN), PLEN)
+        here = pl.ds(pl.multiple_of(p * 128, 128), 128)
         sum_here = total[here, :]
         for k in range(SIDE):
             part = (far_back, far_ahead)[k // 2]
@@ -267,13 +277,14 @@
     return (wide * gain).astype(jnp.bfloat16), lanes(wide * wide)
 
 
-def cross_near_kernel(own, back, ahead, weight, gains, total, square):
+def cross_near_kernel(*refs):
+    parts, (weight, gains, total, square) = refs[:6], refs[6:]
+
     @pl.loop(0, 4)
     def _(p):
         here = pl.ds(pl.multiple_of(p * 128, 128), 128)
         for k in range(12):
-            part = (own, back, ahead)[k // SIDE]
-            block, squares = scaled(part[k % SIDE, here, :], gains[k])
+            block, squares = scaled(parts[k // 2][k % 2, here, :], gains[k])
             term = jnp.dot(block, weight[k], preferred_element_type=jnp.float32)
             total[here, :] = term if k == 0 else total[here, :] + term
             square[here, :] = squares if k == 0 else square[here, :] + squares
@@ -413,11 +424,11 @@
             arrange_kernel, bf16(BLOCKS, HD, width), [SMEM] + [ANY] * 7, [dma], 0, 4 * D * width
         )(place, *weight)
 
-    parts = gather_halved(attended)
+    near, far = gather_split(attended)
     weight = arrange(outer)
     total = call(
-        residual_near_kernel, f32(tokens, HD), [VMEM] * 5, [], 2 * tokens * D * HD, 6 << 20
-    )(*parts[:3], weight, embedded)
+        residual_near_kernel, f32(tokens, HD), [VMEM] * 8, [], 2 * tokens * D * HD, 6 << 20
+    )(*near, weight, embedded)
     hidden = call(
         residual_far_kernel,
         bf16(tokens, HD),
@@ -425,17 +436,17 @@
         [vmem(SIDE, HD, HD), pltpu.SemaphoreType.DMA],
         tokens * D * HD // 2,
         2 << 20,
-    )(*parts[3:], weight, total)
-    parts = gather_halved(hidden)
+    )(*far, weight, total)
+    near, far = gather_split(hidden)
     weight = arrange(cross)
     total, square = call(
         cross_near_kernel,
         (f32(tokens, 2 * HD), f32(tokens, 128)),
-        [VMEM] * 5,
+        [VMEM] * 8,
         [],
         4 * tokens * D * HD,
         8 << 20,
-    )(*parts[:3], weight, gains)
+    )(*near, weight, gains)
     keys, values = call(
         cross_far_kernel,
         (bf16(tokens, HD), bf16(tokens, HD)),
@@ -443,7 +454,7 @@
         [vmem(SIDE, HD, 2 * HD), pltpu.SemaphoreType.DMA],
         tokens * D * HD,
         3 << 20,
-    )(*parts[3:], weight, gains, total, square)
+    )(*far, weight, gains, total, square)
     return hidden, keys.reshape(tokens, 1, HD), values.reshape(tokens, 1, HD)
 
 

time: 167 us -> 168 us (level)
  the two profiles are of different devices: /device:TPU:1 before, /device:TPU:6 now
where the time goes in v1:
time: 168 us
  waiting for transfers between devices  66.8 us (40%)
  starting transfers between devices  54.2 us (32%)
  Pallas kernels  31.4 us (19%)
  local copies, waits for them, and re-layouts  8.64 us (5%)
  other arithmetic  5.48 us (3%)
    ppermute x42, waiting for transfers between devices, send(): return lax.ppermute(block, ('row', 'col'), moves(step))  66.8 us
    ppermute x42, starting transfers between devices, send(): return lax.ppermute(block, ('row', 'col'), moves(step))  54.2 us
    pallas_call x1, Pallas kernels, body(): call(project_kernel, f32(tokens, 3 * HD), [VMEM] + [ANY] * 6, [vmem(14, H...  6.72 us
    gather x1, local copies, waits for them, and re-layouts, body(): embedded = embedding.at[token_ids.reshape(-1)].get(mode='promise_in_bounds')  6.31 us
    pallas_call x2, Pallas kernels, arrange(): call(arrange_kernel, bf16(BLOCKS, HD, width), [SMEM] + [ANY] * 7, [dma],...  5.5 us
    pallas_call x1, Pallas kernels, body(): call(prepare_kernel, (bf16(tokens, D), f32(tokens, 128), f32(BLOCKS, 1, H...  4.33 us
    pallas_call x2, Pallas kernels, side_by_side(): call(join_kernel, bf16(HD, len(shards) * HD), [HBM] * len(shards), [pltpu...  3.62 us
  transfers between devices with their start and end apart: 42, of which 18 were waited for; matrix products, arithmetic and copies ran while one was open for 7% of the time, Pallas kernels for 16%

profile of v1, /device:TPU:6, one launch (start us, length us, event | category | flops | bytes accessed | tf_op | source)
XLA Modules:
  0.0 167.9 jit_solution(16629054456093272627)
XLA Ops:
  9.5 3.9 %collective-permute-start.20 = (bf16[256,768]{1,0:T(8,128)(2,1)}, bf16[256,768]{1,0:T(8,128)(2,1)S(1)}, u32[]{:S(2)}, u32[]{:S(2)}) collective-permute-start(bf16[256,768]{1,0:T(8,128)(2,1)} %shard_map.135), channel_id=1, source_target_pairs={{0,16},{1,17},{2,18},{3,19},{4,20},{5,21},{6,22},{7,23},{8,24},{9,... | collective-permute-start | bytes 1179656 | tf_op jit(solution)/shard_map/ppermute | solution.py:43
  13.4 8.2 %collective-permute-done.7.hop1 = bf16[2,256,768]{2,1,0:T(8,128)(2,1)S(1)} collective-permute-done((bf16[2,256,768]{2,1,0:T(8,128)(2,1)S(1)}, bf16[2,256,768]{2,1,0:T(8,128)(2,1)S(1)}, u32[]{:S(2)}, u32[]{:S(2)}) %collective-permute-start.7) | collective-permute-done | bytes 786464 | tf_op jit(solution)/shard_map/ppermute | solution.py:43
  21.7 6.3 %gather_fusion = bf16[512,256]{1,0:T(8,128)(2,1)S(1)} fusion(bf16[16384,256]{1,0:T(8,128)(2,1)} %param.13, s32[1024]{0:T(1024)S(1)} %pad_clamp_fusion), kind=kCustom, calls=%fused_computation | custom fusion | bytes 526336 | tf_op jit(solution)/shard_map/gather | solution.py:387
  32.5 2.5 %collective-permute-done.8.hop2 = bf16[2,256,768]{2,1,0:T(8,128)(2,1)} collective-permute-done((bf16[2,256,768]{2,1,0:T(8,128)(2,1)S(1)}, bf16[2,256,768]{2,1,0:T(8,128)(2,1)}, u32[]{:S(2)}, u32[]{:S(2)}) %collective-permute-start.8) | collective-permute-done | bytes 786464 | tf_op jit(solution)/shard_map/ppermute | solution.py:43
  35.7 3.6 %collective-permute-done.21.refs_3_ = bf16[2,256,256]{2,1,0:T(8,128)(2,1)S(1)} collective-permute-done((bf16[2,256,256]{2,1,0:T(8,128)(2,1)S(1)}, bf16[2,256,256]{2,1,0:T(8,128)(2,1)S(1)}, u32[]{:S(2)}, u32[]{:S(2)}) %collective-permute-start.21) | collective-permute-done | bytes 262176 | tf_op jit(solution)/shard_map/ppermute | solution.py:43
  45.9 5.2 %collective-permute-done.22.refs_4_ = bf16[2,256,256]{2,1,0:T(8,128)(2,1)S(1)} collective-permute-done((bf16[2,256,256]{2,1,0:T(8,128)(2,1)S(1)}, bf16[2,256,256]{2,1,0:T(8,128)(2,1)S(1)}, u32[]{:S(2)}, u32[]{:S(2)}) %collective-permute-start.22) | collective-permute-done | bytes 262176 | tf_op jit(solution)/shard_map/ppermute | solution.py:43
  51.9 3.2 %collective-permute-start.5 = (bf16[4,528,256]{2,1,0:T(8,128)(2,1)S(1)}, bf16[4,528,256]{2,1,0:T(8,128)(2,1)}, u32[]{:S(2)}, u32[]{:S(2)}) collective-permute-start(bf16[4,528,256]{2,1,0:T(8,128)(2,1)S(1)} %pad_maximum_fusion.2.own), channel_id=1, source_target_pairs={{0,2},{1,3},{2,0},{3,1},{4,6},{5,7},{6,4},{7,5},{8,10},{9,11},{10,... | collective-permute-start | bytes 3244040 | tf_op jit(solution)/shard_map/ppermute | solution.py:43
  59.2 5.3 %collective-permute-done.23.refs_5_ = bf16[2,256,256]{2,1,0:T(8,128)(2,1)S(1)} collective-permute-done((bf16[2,256,256]{2,1,0:T(8,128)(2,1)}, bf16[2,256,256]{2,1,0:T(8,128)(2,1)S(1)}, u32[]{:S(2)}, u32[]{:S(2)}) %collective-permute-start.23) | collective-permute-done | bytes 262176 | tf_op jit(solution)/shard_map/ppermute | solution.py:43
  69.8 4.6 %collective-permute-done.11.far = bf16[256,768]{1,0:T(8,128)(2,1)S(1)} collective-permute-done((bf16[256,768]{1,0:T(8,128)(2,1)S(1)}, bf16[256,768]{1,0:T(8,128)(2,1)S(1)}, u32[]{:S(2)}, u32[]{:S(2)}) %collective-permute-start.11) | collective-permute-done | bytes 393248 | tf_op jit(solution)/shard_map/ppermute | solution.py:43
  74.4 4.3 %shard_map.131 = (bf16[512,4096]{1,0:T(8,128)(2,1)S(1)}, f32[512,128]{1,0:T(8,128)S(1)}, f32[16,1,256]{2,1,0:T(1,128)S(1)}) custom-call(s32[2]{0:T(128)S(1)} %pad_add_fusion.place_ref.refs_0_, bf16[4,528,256]{2,1,0:T(8,128)(2,1)S(1)} %pad_maximum_fusion.2.own, bf16[4,528,256]{2,1,0:T(8,128)(2,1)} %collective-permute-done.3.back, ...), custom_call_target="tpu_custom_call" | custom-call | flops 53687091200 | bytes 8388608 | tf_op jit(solution)/shard_map/pallas_call | solution.py:392
  78.8 6.7 %shard_map.133.total = f32[512,768]{1,0:T(8,128)S(1)} custom-call(bf16[512,4096]{1,0:T(8,128)(2,1)S(1)} %get-tuple-element.10.rows, bf16[256,768]{1,0:T(8,128)(2,1)S(1)} %copy-done, bf16[256,768]{1,0:T(8,128)(2,1)S(1)} %copy-done.11, bf16[2,256,768]{2,1,0:T(8,128)(2,1)S(1)} %copy-done.9, bf16[2,256,768]{2,1,0:T(8,128)(2,1)} %collective-permute-done.8.hop2, ...), custom_call_target="tpu_custom_call" | custom-call | flops 3221225472 | bytes 10485760 | tf_op jit(solution)/shard_map/pallas_call | solution.py:400
  85.6 3.3 %shard_map.134 = bf16[512,256]{1,0:T(8,128)(2,1)S(1)} custom-call(s32[2]{0:T(128)S(1)} %copy-done.12, bf16[512,4096]{1,0:T(8,128)(2,1)S(1)} %get-tuple-element.10.rows, f32[512,128]{1,0:T(8,128)S(1)} %get-tuple-element.11.square, f32[512,768]{1,0:T(8,128)S(1)} %shard_map.133.total, bf16[256,768]{1,0:T(8,128)(2,1)S(1)} %collective-permute-done.11.far, ...), custom_call_target="tpu_custom_call" | custom-call | flops 536870912 | bytes 4194304 | tf_op jit(solution)/shard_map/pallas_call | solution.py:408
  94.0 5.3 %collective-permute-done.16 = bf16[512,256]{1,0:T(8,128)(2,1)S(1)} collective-permute-done((bf16[512,256]{1,0:T(8,128)(2,1)S(1)}, bf16[512,256]{1,0:T(8,128)(2,1)S(1)}, u32[]{:S(2)}, u32[]{:S(2)}) %collective-permute-start.16) | collective-permute-done | bytes 262176 | tf_op jit(solution)/shard_map/ppermute | solution.py:43
  99.4 3.1 %collective-permute-start.18 = (bf16[2,512,256]{2,1,0:T(8,128)(2,1)S(1)}, bf16[2,512,256]{2,1,0:T(8,128)(2,1)S(1)}, u32[]{:S(2)}, u32[]{:S(2)}) collective-permute-start(bf16[2,512,256]{2,1,0:T(8,128)(2,1)S(1)} %pad_maximum_fusion.6.refs_1_), channel_id=1, source_target_pairs={{0,3},{1,0},{2,1},{3,2},{4,7},{5,4},{6,5},{7,6},{8,11},{9,8},{10,9... | collective-permute-start | bytes 1572872 | tf_op jit(solution)/shard_map/ppermute | solution.py:43
  104.3 6.1 %collective-permute-done.38.refs_6_ = bf16[256,512]{1,0:T(8,128)(2,1)S(1)} collective-permute-done((bf16[256,512]{1,0:T(8,128)(2,1)S(1)}, bf16[256,512]{1,0:T(8,128)(2,1)S(1)}, u32[]{:S(2)}, u32[]{:S(2)}) %collective-permute-start.38) | collective-permute-done | bytes 262176 | tf_op jit(solution)/shard_map/ppermute | solution.py:43
  110.4 3.2 %collective-permute-start.27 = (bf16[2,512,256]{2,1,0:T(8,128)(2,1)S(1)}, bf16[2,512,256]{2,1,0:T(8,128)(2,1)S(1)}, u32[]{:S(2)}, u32[]{:S(2)}) collective-permute-start(bf16[2,512,256]{2,1,0:T(8,128)(2,1)S(1)} %pad_maximum_fusion.5.refs_0_), channel_id=1, source_target_pairs={{0,3},{1,0},{2,1},{3,2},{4,7},{5,4},{6,5},{7,6},{8,11},{9,8},{10,9... | collective-permute-start | bytes 1572872 | tf_op jit(solution)/shard_map/ppermute | solution.py:43
  116.0 4.2 %shard_map.136.refs_6_.weight = bf16[16,256,256]{2,1,0:T(8,128)(2,1)S(1)} custom-call(s32[2]{0:T(128)S(1)} %pad_add_fusion.place_ref.refs_0_, bf16[256,256]{1,0:T(8,128)(2,1)S(1)} %copy-done.1, bf16[256,256]{1,0:T(8,128)(2,1)S(1)} %get-tuple-element.22.refs_2_, bf16[2,256,256]{2,1,0:T(8,128)(2,1)S(1)} %copy-done.5, bf16[2,256,256]{2,1,0:T(8,128)(2,1)S(1)} %copy-done.7, ...), custom_call_target="tpu_custom_call" | custom-call | bytes 4194304 | tf_op jit(solution)/shard_map/pallas_call | solution.py:423
  121.8 4.1 %collective-permute-done.19.far_ahead = bf16[2,512,256]{2,1,0:T(8,128)(2,1)S(1)} collective-permute-done((bf16[2,512,256]{2,1,0:T(8,128)(2,1)S(1)}, bf16[2,512,256]{2,1,0:T(8,128)(2,1)S(1)}, u32[]{:S(2)}, u32[]{:S(2)}) %collective-permute-start.19) | collective-permute-done | bytes 524320 | tf_op jit(solution)/shard_map/ppermute | solution.py:43
  131.4 6.4 %collective-permute-done.31 = bf16[512,256]{1,0:T(8,128)(2,1)S(1)} collective-permute-done((bf16[512,256]{1,0:T(8,128)(2,1)}, bf16[512,256]{1,0:T(8,128)(2,1)S(1)}, u32[]{:S(2)}, u32[]{:S(2)}) %collective-permute-start.31) | collective-permute-done | bytes 262176 | tf_op jit(solution)/shard_map/ppermute | solution.py:43
  138.9 4.0 %collective-permute-start.33 = (bf16[2,512,256]{2,1,0:T(8,128)(2,1)S(1)}, bf16[2,512,256]{2,1,0:T(8,128)(2,1)S(1)}, u32[]{:S(2)}, u32[]{:S(2)}) collective-permute-start(bf16[2,512,256]{2,1,0:T(8,128)(2,1)S(1)} %pad_maximum_fusion.8.refs_1_), channel_id=1, source_target_pairs={{0,3},{1,0},{2,1},{3,2},{4,7},{5,4},{6,5},{7,6},{8,11},{9,8},{10,9... | collective-permute-start | bytes 1572872 | tf_op jit(solution)/shard_map/ppermute | solution.py:43
  149.5 3.7 %collective-permute-start.34 = (bf16[2,512,256]{2,1,0:T(8,128)(2,1)S(1)}, bf16[2,512,256]{2,1,0:T(8,128)(2,1)S(1)}, u32[]{:S(2)}, u32[]{:S(2)}) collective-permute-start(bf16[2,512,256]{2,1,0:T(8,128)(2,1)S(1)} %collective-permute-done.33.refs_5_), channel_id=1, source_target_pairs={{0,3},{1,0},{2,1},{3,2},{4,7},{5,4},{6,5},{7,6},{8,11},{9,8},{10,9... | collective-permute-start | bytes 1572872 | tf_op jit(solution)/shard_map/ppermute | solution.py:43
  155.6 4.3 %collective-permute-done.40.refs_3_ = bf16[2,512,256]{2,1,0:T(8,128)(2,1)S(1)} collective-permute-done((bf16[2,512,256]{2,1,0:T(8,128)(2,1)S(1)}, bf16[2,512,256]{2,1,0:T(8,128)(2,1)S(1)}, u32[]{:S(2)}, u32[]{:S(2)}) %collective-permute-start.40) | collective-permute-done | bytes 524320 | tf_op jit(solution)/shard_map/ppermute | solution.py:43
  159.9 2.5 %shard_map.140 = (f32[512,512]{1,0:T(8,128)S(1)}, f32[512,128]{1,0:T(8,128)S(1)}) custom-call(bf16[2,512,256]{2,1,0:T(8,128)(2,1)S(1)} %pad_maximum_fusion.7.refs_0_, bf16[2,512,256]{2,1,0:T(8,128)(2,1)S(1)} %pad_maximum_fusion.8.refs_1_, bf16[2,512,256]{2,1,0:T(8,128)(2,1)S(1)} %collective-permute-done.29.refs_2_, ...), custom_call_target="tpu_custom_call" | custom-call | flops 2147483648 | bytes 8388608 | tf_op jit(solution)/shard_map/pallas_call | solution.py:442
  162.4 3.1 %collective-permute-done.30.far_back = bf16[2,512,256]{2,1,0:T(8,128)(2,1)S(1)} collective-permute-done((bf16[2,512,256]{2,1,0:T(8,128)(2,1)S(1)}, bf16[2,512,256]{2,1,0:T(8,128)(2,1)S(1)}, u32[]{:S(2)}, u32[]{:S(2)}) %collective-permute-start.30) | collective-permute-done | bytes 524320 | tf_op jit(solution)/shard_map/ppermute | solution.py:43
  (128 shorter events, 59.4 us)
Async XLA Ops:
  5.7 15.9 %collective-permute-start.7 = (bf16[2,256,768]{2,1,0:T(8,128)(2,1)S(1)}, bf16[2,256,768]{2,1,0:T(8,128)(2,1)S(1)}, u32[]{:S(2)}, u32[]{:S(2)}) collective-permute-start(bf16[2,256,768]{2,1,0:T(8,128)(2,1)S(1)} %pad_maximum_fusion.4), channel_id=1, source_target_pairs={{0,32},{1,33},{2,34},{3,35},{4,36},{5,37},{6,38},{7,39},{8,40},{9,... | collective-permute-start | bytes 2359304 | tf_op jit(solution)/shard_map/ppermute | solution.py:43
  9.5 22.0 %collective-permute-start.20 = (bf16[256,768]{1,0:T(8,128)(2,1)}, bf16[256,768]{1,0:T(8,128)(2,1)S(1)}, u32[]{:S(2)}, u32[]{:S(2)}) collective-permute-start(bf16[256,768]{1,0:T(8,128)(2,1)} %shard_map.135), channel_id=1, source_target_pairs={{0,16},{1,17},{2,18},{3,19},{4,20},{5,21},{6,22},{7,23},{8,24},{9,... | collective-permute-start | bytes 1179656 | tf_op jit(solution)/shard_map/ppermute | solution.py:43
  21.6 13.3 %collective-permute-start.8 = (bf16[2,256,768]{2,1,0:T(8,128)(2,1)S(1)}, bf16[2,256,768]{2,1,0:T(8,128)(2,1)}, u32[]{:S(2)}, u32[]{:S(2)}) collective-permute-start(bf16[2,256,768]{2,1,0:T(8,128)(2,1)S(1)} %collective-permute-done.7.hop1), channel_id=1, source_target_pairs={{0,32},{1,33},{2,34},{3,35},{4,36},{5,37},{6,38},{7,39},{8,40},{9,... | collective-permute-start | bytes 2359304 | tf_op jit(solution)/shard_map/ppermute | solution.py:43
  28.0 12.1 %collective-permute-start = (bf16[528,256]{1,0:T(8,128)(2,1)S(1)}, bf16[528,256]{1,0:T(8,128)(2,1)S(1)}, u32[]{:S(2)}, u32[]{:S(2)}) collective-permute-start(bf16[528,256]{1,0:T(8,128)(2,1)S(1)} %shard_map.130), channel_id=1, source_target_pairs={{0,4},{1,5},{2,6},{3,7},{4,8},{5,9},{6,10},{7,11},{8,12},{9,13},{1... | collective-permute-start | bytes 811016 | tf_op jit(solution)/shard_map/ppermute | solution.py:43
  28.6 13.9 %collective-permute-start.1 = (bf16[528,256]{1,0:T(8,128)(2,1)S(1)}, bf16[528,256]{1,0:T(8,128)(2,1)S(1)}, u32[]{:S(2)}, u32[]{:S(2)}) collective-permute-start(bf16[528,256]{1,0:T(8,128)(2,1)S(1)} %shard_map.130), channel_id=1, source_target_pairs={{0,12},{1,13},{2,14},{3,15},{4,0},{5,1},{6,2},{7,3},{8,4},{9,5},{1... | collective-permute-start | bytes 811016 | tf_op jit(solution)/shard_map/ppermute | solution.py:43
  30.1 12.3 %collective-permute-start.2 = (bf16[528,256]{1,0:T(8,128)(2,1)S(1)}, bf16[528,256]{1,0:T(8,128)(2,1)S(1)}, u32[]{:S(2)}, u32[]{:S(2)}) collective-permute-start(bf16[528,256]{1,0:T(8,128)(2,1)S(1)} %shard_map.130), channel_id=1, source_target_pairs={{0,8},{1,9},{2,10},{3,11},{4,12},{5,13},{6,14},{7,15},{8,0},{9,1},... | collective-permute-start | bytes 811016 | tf_op jit(solution)/shard_map/ppermute | solution.py:43
  34.9 21.9 %collective-permute-start.9 = (bf16[2,256,768]{2,1,0:T(8,128)(2,1)}, bf16[2,256,768]{2,1,0:T(8,128)(2,1)S(1)}, u32[]{:S(2)}, u32[]{:S(2)}) collective-permute-start(bf16[2,256,768]{2,1,0:T(8,128)(2,1)} %collective-permute-done.8.hop2), channel_id=1, source_target_pairs={{0,32},{1,33},{2,34},{3,35},{4,36},{5,37},{6,38},{7,39},{8,40},{9,... | collective-permute-start | bytes 2359304 | tf_op jit(solution)/shard_map/ppermute | solution.py:43
  39.3 11.9 %collective-permute-start.22 = (bf16[2,256,256]{2,1,0:T(8,128)(2,1)S(1)}, bf16[2,256,256]{2,1,0:T(8,128)(2,1)S(1)}, u32[]{:S(2)}, u32[]{:S(2)}) collective-permute-start(bf16[2,256,256]{2,1,0:T(8,128)(2,1)S(1)} %collective-permute-done.21.refs_3_), channel_id=1, source_target_pairs={{0,32},{1,33},{2,34},{3,35},{4,36},{5,37},{6,38},{7,39},{8,40},{9,... | collective-permute-start | bytes 786440 | tf_op jit(solution)/shard_map/ppermute | solution.py:43
  40.2 16.6 %collective-permute-start.35 = (bf16[2,256,512]{2,1,0:T(8,128)(2,1)}, bf16[2,256,512]{2,1,0:T(8,128)(2,1)S(1)}, u32[]{:S(2)}, u32[]{:S(2)}) collective-permute-start(bf16[2,256,512]{2,1,0:T(8,128)(2,1)} %pad_maximum_fusion.9), channel_id=1, source_target_pairs={{0,32},{1,33},{2,34},{3,35},{4,36},{5,37},{6,38},{7,39},{8,40},{9,... | collective-permute-start | bytes 1572872 | tf_op jit(solution)/shard_map/ppermute | solution.py:43
  42.6 23.6 %collective-permute-start.3 = (bf16[4,528,256]{2,1,0:T(8,128)(2,1)S(1)}, bf16[4,528,256]{2,1,0:T(8,128)(2,1)}, u32[]{:S(2)}, u32[]{:S(2)}) collective-permute-start(bf16[4,528,256]{2,1,0:T(8,128)(2,1)S(1)} %pad_maximum_fusion.2.own), channel_id=1, source_target_pairs={{0,1},{1,2},{2,3},{3,0},{4,5},{5,6},{6,7},{7,4},{8,9},{9,10},{10,1... | collective-permute-start | bytes 3244040 | tf_op jit(solution)/shard_map/ppermute | solution.py:43
  44.3 23.2 %collective-permute-start.4 = (bf16[4,528,256]{2,1,0:T(8,128)(2,1)S(1)}, bf16[4,528,256]{2,1,0:T(8,128)(2,1)}, u32[]{:S(2)}, u32[]{:S(2)}) collective-permute-start(bf16[4,528,256]{2,1,0:T(8,128)(2,1)S(1)} %pad_maximum_fusion.2.own), channel_id=1, source_target_pairs={{0,3},{1,0},{2,1},{3,2},{4,7},{5,4},{6,5},{7,6},{8,11},{9,8},{10,9... | collective-permute-start | bytes 3244040 | tf_op jit(solution)/shard_map/ppermute | solution.py:43
  51.9 22.5 %collective-permute-start.5 = (bf16[4,528,256]{2,1,0:T(8,128)(2,1)S(1)}, bf16[4,528,256]{2,1,0:T(8,128)(2,1)}, u32[]{:S(2)}, u32[]{:S(2)}) collective-permute-start(bf16[4,528,256]{2,1,0:T(8,128)(2,1)S(1)} %pad_maximum_fusion.2.own), channel_id=1, source_target_pairs={{0,2},{1,3},{2,0},{3,1},{4,6},{5,7},{6,4},{7,5},{8,10},{9,11},{10,... | collective-permute-start | bytes 3244040 | tf_op jit(solution)/shard_map/ppermute | solution.py:43
  56.9 35.1 %collective-permute-start.36 = (bf16[2,256,512]{2,1,0:T(8,128)(2,1)S(1)}, bf16[2,256,512]{2,1,0:T(8,128)(2,1)S(1)}, u32[]{:S(2)}, u32[]{:S(2)}) collective-permute-start(bf16[2,256,512]{2,1,0:T(8,128)(2,1)S(1)} %collective-permute-done.35.refs_3_), channel_id=1, source_target_pairs={{0,32},{1,33},{2,34},{3,35},{4,36},{5,37},{6,38},{7,39},{8,40},{9,... | collective-permute-start | bytes 1572872 | tf_op jit(solution)/shard_map/ppermute | solution.py:43
  66.3 27.5 %collective-permute-start.24 = (bf16[256,256]{1,0:T(8,128)(2,1)S(1)}, bf16[256,256]{1,0:T(8,128)(2,1)S(1)}, u32[]{:S(2)}, u32[]{:S(2)}) collective-permute-start(bf16[256,256]{1,0:T(8,128)(2,1)S(1)} %slice_bitcast_fusion.2), channel_id=1, source_target_pairs={{0,32},{1,33},{2,34},{3,35},{4,36},{5,37},{6,38},{7,39},{8,40},{9,... | collective-permute-start | bytes 393224 | tf_op jit(solution)/shard_map/ppermute | solution.py:43
  93.9 21.9 %collective-permute-start.25 = (bf16[7,256,256]{2,1,0:T(8,128)(2,1)S(1)}, bf16[7,256,256]{2,1,0:T(8,128)(2,1)S(1)}, u32[]{:S(2)}, u32[]{:S(2)}) collective-permute-start(bf16[7,256,256]{2,1,0:T(8,128)(2,1)S(1)} %pad_maximum_fusion.3), channel_id=1, source_target_pairs={{0,16},{1,17},{2,18},{3,19},{4,20},{5,21},{6,22},{7,23},{8,24},{9,... | collective-permute-start | bytes 2752520 | tf_op jit(solution)/shard_map/ppermute | solution.py:43
  99.4 14.2 %collective-permute-start.18 = (bf16[2,512,256]{2,1,0:T(8,128)(2,1)S(1)}, bf16[2,512,256]{2,1,0:T(8,128)(2,1)S(1)}, u32[]{:S(2)}, u32[]{:S(2)}) collective-permute-start(bf16[2,512,256]{2,1,0:T(8,128)(2,1)S(1)} %pad_maximum_fusion.6.refs_1_), channel_id=1, source_target_pairs={{0,3},{1,0},{2,1},{3,2},{4,7},{5,4},{6,5},{7,6},{8,11},{9,8},{10,9... | collective-permute-start | bytes 1572872 | tf_op jit(solution)/shard_map/ppermute | solution.py:43
  102.8 17.4 %collective-permute-start.26 = (bf16[2,512,256]{2,1,0:T(8,128)(2,1)S(1)}, bf16[2,512,256]{2,1,0:T(8,128)(2,1)S(1)}, u32[]{:S(2)}, u32[]{:S(2)}) collective-permute-start(bf16[2,512,256]{2,1,0:T(8,128)(2,1)S(1)} %pad_maximum_fusion.6.refs_1_), channel_id=1, source_target_pairs={{0,1},{1,2},{2,3},{3,0},{4,5},{5,6},{6,7},{7,4},{8,9},{9,10},{10,1... | collective-permute-start | bytes 1572872 | tf_op jit(solution)/shard_map/ppermute | solution.py:43
  113.6 12.3 %collective-permute-start.19 = (bf16[2,512,256]{2,1,0:T(8,128)(2,1)S(1)}, bf16[2,512,256]{2,1,0:T(8,128)(2,1)S(1)}, u32[]{:S(2)}, u32[]{:S(2)}) collective-permute-start(bf16[2,512,256]{2,1,0:T(8,128)(2,1)S(1)} %collective-permute-done.18.refs_5_), channel_id=1, source_target_pairs={{0,3},{1,0},{2,1},{3,2},{4,7},{5,4},{6,5},{7,6},{8,11},{9,8},{10,9... | collective-permute-start | bytes 1572872 | tf_op jit(solution)/shard_map/ppermute | solution.py:43
  113.7 12.2 %collective-permute-start.15 = (bf16[2,512,256]{2,1,0:T(8,128)(2,1)S(1)}, bf16[2,512,256]{2,1,0:T(8,128)(2,1)S(1)}, u32[]{:S(2)}, u32[]{:S(2)}) collective-permute-start(bf16[2,512,256]{2,1,0:T(8,128)(2,1)S(1)} %collective-permute-done.14.refs_2_), channel_id=1, source_target_pairs={{0,1},{1,2},{2,3},{3,0},{4,5},{5,6},{6,7},{7,4},{8,9},{9,10},{10,1... | collective-permute-start | bytes 1572872 | tf_op jit(solution)/shard_map/ppermute | solution.py:43
  115.9 38.5 %collective-permute-start.39 = (bf16[7,256,512]{2,1,0:T(8,128)(2,1)S(1)}, bf16[7,256,512]{2,1,0:T(8,128)(2,1)S(1)}, u32[]{:S(2)}, u32[]{:S(2)}) collective-permute-start(bf16[7,256,512]{2,1,0:T(8,128)(2,1)S(1)} %pad_maximum_fusion.1), channel_id=1, source_target_pairs={{0,16},{1,17},{2,18},{3,19},{4,20},{5,21},{6,22},{7,23},{8,24},{9,... | collective-permute-start | bytes 5505032 | tf_op jit(solution)/shard_map/ppermute | solution.py:43
  130.4 12.5 %collective-permute-start.28 = (bf16[512,256]{1,0:T(8,128)(2,1)}, bf16[512,256]{1,0:T(8,128)(2,1)S(1)}, u32[]{:S(2)}, u32[]{:S(2)}) collective-permute-start(bf16[512,256]{1,0:T(8,128)(2,1)} %shard_map.138), channel_id=1, source_target_pairs={{0,4},{1,5},{2,6},{3,7},{4,8},{5,9},{6,10},{7,11},{8,12},{9,13},{1... | collective-permute-start | bytes 786440 | tf_op jit(solution)/shard_map/ppermute | solution.py:43
  143.9 16.0 %collective-permute-start.40 = (bf16[2,512,256]{2,1,0:T(8,128)(2,1)S(1)}, bf16[2,512,256]{2,1,0:T(8,128)(2,1)S(1)}, u32[]{:S(2)}, u32[]{:S(2)}) collective-permute-start(bf16[2,512,256]{2,1,0:T(8,128)(2,1)S(1)} %pad_maximum_fusion.8.refs_1_), channel_id=1, source_target_pairs={{0,1},{1,2},{2,3},{3,0},{4,5},{5,6},{6,7},{7,4},{8,9},{9,10},{10,1... | collective-permute-start | bytes 1572872 | tf_op jit(solution)/shard_map/ppermute | solution.py:43
  145.4 14.6 %collective-permute-start.41 = (bf16[2,512,256]{2,1,0:T(8,128)(2,1)S(1)}, bf16[2,512,256]{2,1,0:T(8,128)(2,1)S(1)}, u32[]{:S(2)}, u32[]{:S(2)}) collective-permute-start(bf16[2,512,256]{2,1,0:T(8,128)(2,1)S(1)} %pad_maximum_fusion.7.refs_0_), channel_id=1, source_target_pairs={{0,3},{1,0},{2,1},{3,2},{4,7},{5,4},{6,5},{7,6},{8,11},{9,8},{10,9... | collective-permute-start | bytes 1572872 | tf_op jit(solution)/shard_map/ppermute | solution.py:43
  149.5 12.9 %collective-permute-start.34 = (bf16[2,512,256]{2,1,0:T(8,128)(2,1)S(1)}, bf16[2,512,256]{2,1,0:T(8,128)(2,1)S(1)}, u32[]{:S(2)}, u32[]{:S(2)}) collective-permute-start(bf16[2,512,256]{2,1,0:T(8,128)(2,1)S(1)} %collective-permute-done.33.refs_5_), channel_id=1, source_target_pairs={{0,3},{1,0},{2,1},{3,2},{4,7},{5,4},{6,5},{7,6},{8,11},{9,8},{10,9... | collective-permute-start | bytes 1572872 | tf_op jit(solution)/shard_map/ppermute | solution.py:43
  (35 other events, 416.9 us)

commit v2 on v1

--- a/solution.py
+++ b/solution.py
@@ -75,6 +75,13 @@
     back_high, ahead_low = second_leg(high, 1), second_leg(low, 3)
     passed = [second_leg(back_low, 1), second_leg(ahead_high, 3)]
     return [low, high, back_low, back_high, ahead_low, ahead_high], passed
+
+
+def gather_halved(chunk):
+    stack = jnp.stack([chunk] + [first_leg(chunk, s) for s in SHIFTS])
+    back, ahead = second_leg(stack, 1), second_leg(stack, 3)
+    passed = [second_leg(back[:2], 1), second_leg(ahead[2:], 3)]
+    return [stack, back, ahead], passed
 
 
 def gather_weight(shard, other, late):
@@ -134,9 +141,8 @@
 
 def block_of(place, first, second):
     c = place[1]
-    away = jnp.where(first == 0, 0, jnp.where(first == 1, 3, first - 1))
-    x = place[2] + away * (1 - c) + OFFSETS[second] * c
-    y = place[3] + away * c + OFFSETS[second] * (1 - c)
+    x = place[2] + OFFSETS[first] * (1 - c) + OFFSETS[second] * c
+    y = place[3] + OFFSETS[first] * c + OFFSETS[second] * (1 - c)
     return lax.rem(x, SIDE) * SIDE + lax.rem(y, SIDE)
 
 
@@ -162,11 +168,8 @@
 def prepare_kernel(place_ref, own, back, ahead, far, rows, square, final_ref):
     place = read(place_ref)
     tokens, step = rows.shape[0], 64
-    square[...] = jnp.zeros_like(square)
     for second, part in enumerate((own, back, ahead, far)):
-
-        @pl.loop(0, SIDE)
-        def _(first):
+        for first in range(SIDE):
             spot = arrival(place, block_of(place, first, second))
             there = pl.ds(pl.multiple_of(spot * HD, HD), HD)
             gains = part[first, pl.ds(tokens, GAIN_ROWS), :].astype(jnp.float32)
@@ -177,7 +180,8 @@
             def _(tile):
                 here = pl.ds(pl.multiple_of(tile * step, step), step)
                 wide = part[first, here, :].astype(jnp.float32)
-                square[here, :] += lanes(wide * wide)
+                total = lanes(wide * wide)
+                square[here, :] = total if second + first == 0 else square[here, :] + total
                 rows[here, there] = (wide * gain).astype(jnp.bfloat16)
 
 
@@ -200,10 +204,10 @@
     wait_all(copies)
     weight = held.reshape(14 * HD, 3 * HD)
 
-    @pl.loop(0, 12)
+    @pl.loop(0, 6)
     def _(n):
-        here = pl.ds(pl.multiple_of(lax.rem(n, 4) * 128, 128), 128)
-        there = pl.ds(pl.multiple_of(lax.div(n, 4) * HD, HD), HD)
+        here = pl.ds(pl.multiple_of(lax.div(n, 3) * PLEN, PLEN), PLEN)
+        there = pl.ds(pl.multiple_of(lax.rem(n, 3) * HD, HD), HD)
         total[here, there] = jnp.dot(
             rows[here, : 14 * HD], weight[:, there], preferred_element_type=jnp.float32
         )
@@ -215,15 +219,12 @@
         here = pl.ds(pl.multiple_of(p * PLEN, PLEN), PLEN)
         mean = jnp.sum(square[here, :], axis=1, keepdims=True) / D
         inverse = lax.rsqrt(mean + epsilon)
-
-        @pl.loop(0, 3)
-        def _(n):
-            there = pl.ds(pl.multiple_of(n * HD, HD), HD)
+        for n in range(3):
+            there = pl.ds(n * HD, HD)
             head = total[here, there]
             head += jnp.dot(rows[here, 14 * HD : 15 * HD], far[:, there], preferred_element_type=jnp.float32)
             head += jnp.dot(rows[here, 15 * HD :], far_crossed[:, there], preferred_element_type=jnp.float32)
             heads[n] = (head * inverse).astype(jnp.bfloat16)
-
         scores = lax.dot_general(
             heads[0], heads[1], (((1,), (1,)), ((), ())), preferred_element_type=jnp.float32
         ) * HD ** (-0.5)
@@ -262,9 +263,9 @@
     load.start()
     load.wait()
 
-    @pl.loop(0, 4)
+    @pl.loop(0, 2)
     def _(p):
-        here = pl.ds(pl.multiple_of(p * 128, 128), 128)
+        here = pl.ds(pl.multiple_of(p * PLEN, PLEN), PLEN)
         sum_here = total[here, :]
         for k in range(SIDE):
             part = (far_back, far_ahead)[k // 2]
@@ -278,13 +279,13 @@
 
 
 def cross_near_kernel(*refs):
-    parts, (weight, gains, total, square) = refs[:6], refs[6:]
+    parts, (weight, gains, total, square) = refs[:3], refs[3:]
 
     @pl.loop(0, 4)
     def _(p):
         here = pl.ds(pl.multiple_of(p * 128, 128), 128)
         for k in range(12):
-            block, squares = scaled(parts[k // 2][k % 2, here, :], gains[k])
+            block, squares = scaled(parts[k // SIDE][k % SIDE, here, :], gains[k])
             term = jnp.dot(block, weight[k], preferred_element_type=jnp.float32)
             total[here, :] = term if k == 0 else total[here, :] + term
             square[here, :] = squares if k == 0 else square[here, :] + squares
@@ -421,7 +422,13 @@
     def arrange(weight):
         width = weight[0].shape[1]
         return call(
-            arrange_kernel, bf16(BLOCKS, HD, width), [SMEM] + [ANY] * 7, [dma], 0, 4 * D * width
+            arrange_kernel,
+            bf16(BLOCKS, HD, width),
+            [SMEM] + [ANY] * 7,
+            [dma],
+            0,
+            4 * D * width,
+            grant=58,
         )(place, *weight)
 
     near, far = gather_split(attended)
@@ -437,12 +444,12 @@
         tokens * D * HD // 2,
         2 << 20,
     )(*far, weight, total)
-    near, far = gather_split(hidden)
+    near, far = gather_halved(hidden)
     weight = arrange(cross)
     total, square = call(
         cross_near_kernel,
         (f32(tokens, 2 * HD), f32(tokens, 128)),
-        [VMEM] * 8,
+        [VMEM] * 5,
         [],
         4 * tokens * D * HD,
         8 << 20,

time: 168 us -> 170 us (1.012)
  the two profiles are of different devices: /device:TPU:6 before, /device:TPU:1 now
where the time goes in v2:
time: 170 us; the launch traced here: 169 us
  waiting for transfers between devices  61.9 us (36%)
  starting transfers between devices  52.5 us (31%)
  Pallas kernels  31.5 us (19%)
  local copies, waits for them, and re-layouts  13.9 us (8%)
  other arithmetic  7.43 us (4%)
    ppermute x40, waiting for transfers between devices, send(): return lax.ppermute(block, ('row', 'col'), moves(step))  61.9 us
    ppermute x40, starting transfers between devices, send(): return lax.ppermute(block, ('row', 'col'), moves(step))  52.5 us
    pallas_call x2, Pallas kernels, arrange(): call(arrange_kernel, bf16(BLOCKS, HD, width), [SMEM] + [ANY] * 7, [dma],...  8.89 us
    gather x1, local copies, waits for them, and re-layouts, body(): embedded = embedding.at[token_ids.reshape(-1)].get(mode='promise_in_bounds')  6.07 us
    pallas_call x1, Pallas kernels, body(): call(project_kernel, f32(tokens, 3 * HD), [VMEM] + [ANY] * 6, [vmem(14, H...  5.56 us
    unnamed x43, local copies, waits for them, and re-layouts  5.51 us
    pallas_call x1, Pallas kernels, body(): call(prepare_kernel, (bf16(tokens, D), f32(tokens, 128), f32(BLOCKS, 1, H...  3.88 us
    pallas_call x2, Pallas kernels, side_by_side(): call(join_kernel, bf16(HD, len(shards) * HD), [HBM] * len(shards), [pltpu...  3.64 us
  transfers between devices with their start and end apart: 40, of which 17 were waited for; matrix products, arithmetic and copies ran while one was open for 9% of the time, Pallas kernels for 16%

profile of v2, /device:TPU:1, one launch (start us, length us, event | category | flops | bytes accessed | tf_op | source)
XLA Modules:
  0.0 168.5 jit_solution(1562409528844173770)
XLA Ops:
  2.5 3.3 %collective-permute-start.6 = (bf16[256,768]{1,0:T(8,128)(2,1)}, bf16[256,768]{1,0:T(8,128)(2,1)S(1)}, u32[]{:S(2)}, u32[]{:S(2)}) collective-permute-start(bf16[256,768]{1,0:T(8,128)(2,1)} %shard_map.132.own), channel_id=1, source_target_pairs={{0,16},{1,17},{2,18},{3,19},{4,20},{5,21},{6,22},{7,23},{8,24},{9,... | collective-permute-start | bytes 1179656 | tf_op jit(solution)/shard_map/ppermute | solution.py:43
  8.4 3.9 %collective-permute-start.7 = (bf16[2,256,768]{2,1,0:T(8,128)(2,1)S(1)}, bf16[2,256,768]{2,1,0:T(8,128)(2,1)S(1)}, u32[]{:S(2)}, u32[]{:S(2)}) collective-permute-start(bf16[2,256,768]{2,1,0:T(8,128)(2,1)S(1)} %pad_maximum_fusion.5), channel_id=1, source_target_pairs={{0,32},{1,33},{2,34},{3,35},{4,36},{5,37},{6,38},{7,39},{8,40},{9,... | collective-permute-start | bytes 2359304 | tf_op jit(solution)/shard_map/ppermute | solution.py:43
  14.3 7.0 %collective-permute-done.7.hop1 = bf16[2,256,768]{2,1,0:T(8,128)(2,1)S(1)} collective-permute-done((bf16[2,256,768]{2,1,0:T(8,128)(2,1)S(1)}, bf16[2,256,768]{2,1,0:T(8,128)(2,1)S(1)}, u32[]{:S(2)}, u32[]{:S(2)}) %collective-permute-start.7) | collective-permute-done | bytes 786464 | tf_op jit(solution)/shard_map/ppermute | solution.py:43
  21.3 3.1 %collective-permute-start.8 = (bf16[2,256,768]{2,1,0:T(8,128)(2,1)S(1)}, bf16[2,256,768]{2,1,0:T(8,128)(2,1)}, u32[]{:S(2)}, u32[]{:S(2)}) collective-permute-start(bf16[2,256,768]{2,1,0:T(8,128)(2,1)S(1)} %collective-permute-done.7.hop1), channel_id=1, source_target_pairs={{0,32},{1,33},{2,34},{3,35},{4,36},{5,37},{6,38},{7,39},{8,40},{9,... | collective-permute-start | bytes 2359304 | tf_op jit(solution)/shard_map/ppermute | solution.py:43
  24.4 6.1 %gather_fusion = bf16[512,256]{1,0:T(8,128)(2,1)S(1)} fusion(bf16[16384,256]{1,0:T(8,128)(2,1)} %param.13, s32[1024]{0:T(1024)S(1)} %pad_clamp_fusion), kind=kCustom, calls=%fused_computation | custom fusion | bytes 526336 | tf_op jit(solution)/shard_map/gather | solution.py:388
  37.9 3.5 %collective-permute-done.21.refs_3_ = bf16[2,256,256]{2,1,0:T(8,128)(2,1)S(1)} collective-permute-done((bf16[2,256,256]{2,1,0:T(8,128)(2,1)S(1)}, bf16[2,256,256]{2,1,0:T(8,128)(2,1)S(1)}, u32[]{:S(2)}, u32[]{:S(2)}) %collective-permute-start.21) | collective-permute-done | bytes 262176 | tf_op jit(solution)/shard_map/ppermute | solution.py:43
  46.4 6.3 %collective-permute-done.22.refs_4_ = bf16[2,256,256]{2,1,0:T(8,128)(2,1)S(1)} collective-permute-done((bf16[2,256,256]{2,1,0:T(8,128)(2,1)S(1)}, bf16[2,256,256]{2,1,0:T(8,128)(2,1)S(1)}, u32[]{:S(2)}, u32[]{:S(2)}) %collective-permute-start.22) | collective-permute-done | bytes 262176 | tf_op jit(solution)/shard_map/ppermute | solution.py:43
  53.4 2.7 %collective-permute-start.5 = (bf16[4,528,256]{2,1,0:T(8,128)(2,1)S(1)}, bf16[4,528,256]{2,1,0:T(8,128)(2,1)}, u32[]{:S(2)}, u32[]{:S(2)}) collective-permute-start(bf16[4,528,256]{2,1,0:T(8,128)(2,1)S(1)} %pad_maximum_fusion.2.own), channel_id=1, source_target_pairs={{0,2},{1,3},{2,0},{3,1},{4,6},{5,7},{6,4},{7,5},{8,10},{9,11},{10,... | collective-permute-start | bytes 3244040 | tf_op jit(solution)/shard_map/ppermute | solution.py:43
  59.7 4.5 %collective-permute-done.23.refs_5_ = bf16[2,256,256]{2,1,0:T(8,128)(2,1)S(1)} collective-permute-done((bf16[2,256,256]{2,1,0:T(8,128)(2,1)}, bf16[2,256,256]{2,1,0:T(8,128)(2,1)S(1)}, u32[]{:S(2)}, u32[]{:S(2)}) %collective-permute-start.23) | collective-permute-done | bytes 262176 | tf_op jit(solution)/shard_map/ppermute | solution.py:43
  70.9 3.1 %collective-permute-done.11.far = bf16[256,768]{1,0:T(8,128)(2,1)S(1)} collective-permute-done((bf16[256,768]{1,0:T(8,128)(2,1)S(1)}, bf16[256,768]{1,0:T(8,128)(2,1)S(1)}, u32[]{:S(2)}, u32[]{:S(2)}) %collective-permute-start.11) | collective-permute-done | bytes 393248 | tf_op jit(solution)/shard_map/ppermute | solution.py:43
  74.0 3.3 %collective-permute-start.12 = (bf16[256,768]{1,0:T(8,128)(2,1)S(1)}, bf16[256,768]{1,0:T(8,128)(2,1)S(1)}, u32[]{:S(2)}, u32[]{:S(2)}) collective-permute-start(bf16[256,768]{1,0:T(8,128)(2,1)S(1)} %collective-permute-done.11.far), channel_id=1, source_target_pairs={{0,16},{1,17},{2,18},{3,19},{4,20},{5,21},{6,22},{7,23},{8,24},{9,... | collective-permute-start | bytes 1179656 | tf_op jit(solution)/shard_map/ppermute | solution.py:43
  77.3 3.9 %shard_map.131 = (bf16[512,4096]{1,0:T(8,128)(2,1)S(1)}, f32[512,128]{1,0:T(8,128)S(1)}, f32[16,1,256]{2,1,0:T(1,128)S(1)}) custom-call(s32[2]{0:T(128)S(1)} %pad_add_fusion.place_ref.refs_0_, bf16[4,528,256]{2,1,0:T(8,128)(2,1)S(1)} %pad_maximum_fusion.2.own, bf16[4,528,256]{2,1,0:T(8,128)(2,1)} %collective-permute-done.3.back, ...), custom_call_target="tpu_custom_call" | custom-call | flops 53687091200 | bytes 8388608 | tf_op jit(solution)/shard_map/pallas_call | solution.py:393
  81.8 5.6 %shard_map.133.total = f32[512,768]{1,0:T(8,128)S(1)} custom-call(bf16[512,4096]{1,0:T(8,128)(2,1)S(1)} %get-tuple-element.10.rows, bf16[256,768]{1,0:T(8,128)(2,1)S(1)} %copy-done.3, bf16[256,768]{1,0:T(8,128)(2,1)S(1)} %collective-permute-done.6.other, bf16[2,256,768]{2,1,0:T(8,128)(2,1)S(1)} %collective-permute-done.7.hop1, ...), custom_call_target="tpu_custom_call" | custom-call | flops 3221225472 | bytes 10485760 | tf_op jit(solution)/shard_map/pallas_call | solution.py:401
  89.6 2.8 %collective-permute-start.16 = (bf16[512,256]{1,0:T(8,128)(2,1)S(1)}, bf16[512,256]{1,0:T(8,128)(2,1)S(1)}, u32[]{:S(2)}, u32[]{:S(2)}) collective-permute-start(bf16[512,256]{1,0:T(8,128)(2,1)S(1)} %shard_map.134), channel_id=1, source_target_pairs={{0,12},{1,13},{2,14},{3,15},{4,0},{5,1},{6,2},{7,3},{8,4},{9,5},{1... | collective-permute-start | bytes 786440 | tf_op jit(solution)/shard_map/ppermute | solution.py:43
  93.7 4.8 %collective-permute-done.16 = bf16[512,256]{1,0:T(8,128)(2,1)S(1)} collective-permute-done((bf16[512,256]{1,0:T(8,128)(2,1)S(1)}, bf16[512,256]{1,0:T(8,128)(2,1)S(1)}, u32[]{:S(2)}, u32[]{:S(2)}) %collective-permute-start.16) | collective-permute-done | bytes 262176 | tf_op jit(solution)/shard_map/ppermute | solution.py:43
  103.8 4.2 %collective-permute-done.38.refs_6_ = bf16[256,512]{1,0:T(8,128)(2,1)S(1)} collective-permute-done((bf16[256,512]{1,0:T(8,128)(2,1)S(1)}, bf16[256,512]{1,0:T(8,128)(2,1)S(1)}, u32[]{:S(2)}, u32[]{:S(2)}) %collective-permute-start.38) | collective-permute-done | bytes 262176 | tf_op jit(solution)/shard_map/ppermute | solution.py:43
  115.3 3.0 %collective-permute-start.39 = (bf16[7,256,512]{2,1,0:T(8,128)(2,1)}, bf16[7,256,512]{2,1,0:T(8,128)(2,1)}, u32[]{:S(2)}, u32[]{:S(2)}) collective-permute-start(bf16[7,256,512]{2,1,0:T(8,128)(2,1)} %pad_maximum_fusion.1), channel_id=1, source_target_pairs={{0,16},{1,17},{2,18},{3,19},{4,20},{5,21},{6,22},{7,23},{8,24},{9,... | collective-permute-start | bytes 5505032 | tf_op jit(solution)/shard_map/ppermute | solution.py:43
  118.4 3.9 %shard_map.136.refs_6_.weight = bf16[16,256,256]{2,1,0:T(8,128)(2,1)} custom-call(s32[2]{0:T(128)} %copy-done.4, bf16[256,256]{1,0:T(8,128)(2,1)} %refs_1_.5, bf16[256,256]{1,0:T(8,128)(2,1)} %get-tuple-element.22.refs_2_, bf16[2,256,256]{2,1,0:T(8,128)(2,1)} %copy-done.14, bf16[2,256,256]{2,1,0:T(8,128)(2,1)} %copy-done.16, ...), custom_call_target="tpu_custom_call" | custom-call | bytes 4194304 | tf_op jit(solution)/shard_map/pallas_call | solution.py:424
  126.9 2.7 %collective-permute-start.29 = (bf16[512,256]{1,0:T(8,128)(2,1)}, bf16[512,256]{1,0:T(8,128)(2,1)S(1)}, u32[]{:S(2)}, u32[]{:S(2)}) collective-permute-start(bf16[512,256]{1,0:T(8,128)(2,1)} %shard_map.138), channel_id=1, source_target_pairs={{0,12},{1,13},{2,14},{3,15},{4,0},{5,1},{6,2},{7,3},{8,4},{9,5},{1... | collective-permute-start | bytes 786440 | tf_op jit(solution)/shard_map/ppermute | solution.py:43
  130.3 3.5 %collective-permute-done.28 = bf16[512,256]{1,0:T(8,128)(2,1)S(1)} collective-permute-done((bf16[512,256]{1,0:T(8,128)(2,1)}, bf16[512,256]{1,0:T(8,128)(2,1)S(1)}, u32[]{:S(2)}, u32[]{:S(2)}) %collective-permute-start.28) | collective-permute-done | bytes 262176 | tf_op jit(solution)/shard_map/ppermute | solution.py:43
  138.5 2.7 %collective-permute-start.33 = (bf16[4,512,256]{2,1,0:T(8,128)(2,1)S(1)}, bf16[4,512,256]{2,1,0:T(8,128)(2,1)S(1)}, u32[]{:S(2)}, u32[]{:S(2)}) collective-permute-start(bf16[4,512,256]{2,1,0:T(8,128)(2,1)S(1)} %pad_maximum_fusion.3.refs_0_), channel_id=1, source_target_pairs={{0,3},{1,0},{2,1},{3,2},{4,7},{5,4},{6,5},{7,6},{8,11},{9,8},{10,9... | collective-permute-start | bytes 3145736 | tf_op jit(solution)/shard_map/ppermute | solution.py:43
  141.2 12.5 %collective-permute-done.31.refs_1_ = bf16[4,512,256]{2,1,0:T(8,128)(2,1)S(1)} collective-permute-done((bf16[4,512,256]{2,1,0:T(8,128)(2,1)S(1)}, bf16[4,512,256]{2,1,0:T(8,128)(2,1)S(1)}, u32[]{:S(2)}, u32[]{:S(2)}) %collective-permute-start.31) | collective-permute-done | bytes 1048608 | tf_op jit(solution)/shard_map/ppermute | solution.py:43
  153.9 2.7 %collective-permute-start.34 = (bf16[2,512,256]{2,1,0:T(8,128)(2,1)S(1)}, bf16[2,512,256]{2,1,0:T(8,128)(2,1)S(1)}, u32[]{:S(2)}, u32[]{:S(2)}) collective-permute-start(bf16[2,512,256]{2,1,0:T(8,128)(2,1)S(1)} %slice.38), channel_id=1, source_target_pairs={{0,3},{1,0},{2,1},{3,2},{4,7},{5,4},{6,5},{7,6},{8,11},{9,8},{10,9... | collective-permute-start | bytes 1572872 | tf_op jit(solution)/shard_map/ppermute | solution.py:43
  156.6 5.0 %shard_map.139.refs_3_.weight = bf16[16,256,512]{2,1,0:T(8,128)(2,1)} custom-call(s32[2]{0:T(128)} %copy-done.4, bf16[256,512]{1,0:T(8,128)(2,1)} %get-tuple-element.18.refs_1_, bf16[256,512]{1,0:T(8,128)(2,1)} %get-tuple-element.20.refs_2_, bf16[2,256,512]{2,1,0:T(8,128)(2,1)} %collective-permute-done.35.refs_3_, bf16[2,256,512]{2,1,0:T(8,128)(2,1)} %copy-done.9, ...), custom_call_target="tpu_custom_call" | custom-call | bytes 8388608 | tf_op jit(solution)/shard_map/pallas_call | solution.py:424
  (133 shorter events, 63.2 us)
Async XLA Ops:
  8.4 12.9 %collective-permute-start.7 = (bf16[2,256,768]{2,1,0:T(8,128)(2,1)S(1)}, bf16[2,256,768]{2,1,0:T(8,128)(2,1)S(1)}, u32[]{:S(2)}, u32[]{:S(2)}) collective-permute-start(bf16[2,256,768]{2,1,0:T(8,128)(2,1)S(1)} %pad_maximum_fusion.5), channel_id=1, source_target_pairs={{0,32},{1,33},{2,34},{3,35},{4,36},{5,37},{6,38},{7,39},{8,40},{9,... | collective-permute-start | bytes 2359304 | tf_op jit(solution)/shard_map/ppermute | solution.py:43
  14.2 20.8 %collective-permute-start.20 = (bf16[256,768]{1,0:T(8,128)(2,1)}, bf16[256,768]{1,0:T(8,128)(2,1)S(1)}, u32[]{:S(2)}, u32[]{:S(2)}) collective-permute-start(bf16[256,768]{1,0:T(8,128)(2,1)} %shard_map.135), channel_id=1, source_target_pairs={{0,16},{1,17},{2,18},{3,19},{4,20},{5,21},{6,22},{7,23},{8,24},{9,... | collective-permute-start | bytes 1179656 | tf_op jit(solution)/shard_map/ppermute | solution.py:43
  21.3 15.3 %collective-permute-start.8 = (bf16[2,256,768]{2,1,0:T(8,128)(2,1)S(1)}, bf16[2,256,768]{2,1,0:T(8,128)(2,1)}, u32[]{:S(2)}, u32[]{:S(2)}) collective-permute-start(bf16[2,256,768]{2,1,0:T(8,128)(2,1)S(1)} %collective-permute-done.7.hop1), channel_id=1, source_target_pairs={{0,32},{1,33},{2,34},{3,35},{4,36},{5,37},{6,38},{7,39},{8,40},{9,... | collective-permute-start | bytes 2359304 | tf_op jit(solution)/shard_map/ppermute | solution.py:43
  30.6 12.8 %collective-permute-start = (bf16[528,256]{1,0:T(8,128)(2,1)S(1)}, bf16[528,256]{1,0:T(8,128)(2,1)S(1)}, u32[]{:S(2)}, u32[]{:S(2)}) collective-permute-start(bf16[528,256]{1,0:T(8,128)(2,1)S(1)} %shard_map.130), channel_id=1, source_target_pairs={{0,4},{1,5},{2,6},{3,7},{4,8},{5,9},{6,10},{7,11},{8,12},{9,13},{1... | collective-permute-start | bytes 811016 | tf_op jit(solution)/shard_map/ppermute | solution.py:43
  36.6 23.0 %collective-permute-start.9 = (bf16[2,256,768]{2,1,0:T(8,128)(2,1)}, bf16[2,256,768]{2,1,0:T(8,128)(2,1)S(1)}, u32[]{:S(2)}, u32[]{:S(2)}) collective-permute-start(bf16[2,256,768]{2,1,0:T(8,128)(2,1)} %collective-permute-done.8.hop2), channel_id=1, source_target_pairs={{0,32},{1,33},{2,34},{3,35},{4,36},{5,37},{6,38},{7,39},{8,40},{9,... | collective-permute-start | bytes 2359304 | tf_op jit(solution)/shard_map/ppermute | solution.py:43
  43.4 14.9 %collective-permute-start.35 = (bf16[2,256,512]{2,1,0:T(8,128)(2,1)}, bf16[2,256,512]{2,1,0:T(8,128)(2,1)}, u32[]{:S(2)}, u32[]{:S(2)}) collective-permute-start(bf16[2,256,512]{2,1,0:T(8,128)(2,1)} %pad_maximum_fusion.8), channel_id=1, source_target_pairs={{0,32},{1,33},{2,34},{3,35},{4,36},{5,37},{6,38},{7,39},{8,40},{9,... | collective-permute-start | bytes 1572872 | tf_op jit(solution)/shard_map/ppermute | solution.py:43
  43.6 24.4 %collective-permute-start.3 = (bf16[4,528,256]{2,1,0:T(8,128)(2,1)S(1)}, bf16[4,528,256]{2,1,0:T(8,128)(2,1)}, u32[]{:S(2)}, u32[]{:S(2)}) collective-permute-start(bf16[4,528,256]{2,1,0:T(8,128)(2,1)S(1)} %pad_maximum_fusion.2.own), channel_id=1, source_target_pairs={{0,1},{1,2},{2,3},{3,0},{4,5},{5,6},{6,7},{7,4},{8,9},{9,10},{10,1... | collective-permute-start | bytes 3244040 | tf_op jit(solution)/shard_map/ppermute | solution.py:43
  44.7 25.3 %collective-permute-start.4 = (bf16[4,528,256]{2,1,0:T(8,128)(2,1)S(1)}, bf16[4,528,256]{2,1,0:T(8,128)(2,1)}, u32[]{:S(2)}, u32[]{:S(2)}) collective-permute-start(bf16[4,528,256]{2,1,0:T(8,128)(2,1)S(1)} %pad_maximum_fusion.2.own), channel_id=1, source_target_pairs={{0,3},{1,0},{2,1},{3,2},{4,7},{5,4},{6,5},{7,6},{8,11},{9,8},{10,9... | collective-permute-start | bytes 3244040 | tf_op jit(solution)/shard_map/ppermute | solution.py:43
  53.4 23.9 %collective-permute-start.5 = (bf16[4,528,256]{2,1,0:T(8,128)(2,1)S(1)}, bf16[4,528,256]{2,1,0:T(8,128)(2,1)}, u32[]{:S(2)}, u32[]{:S(2)}) collective-permute-start(bf16[4,528,256]{2,1,0:T(8,128)(2,1)S(1)} %pad_maximum_fusion.2.own), channel_id=1, source_target_pairs={{0,2},{1,3},{2,0},{3,1},{4,6},{5,7},{6,4},{7,5},{8,10},{9,11},{10,... | collective-permute-start | bytes 3244040 | tf_op jit(solution)/shard_map/ppermute | solution.py:43
  59.6 21.5 %collective-permute-start.36 = (bf16[2,256,512]{2,1,0:T(8,128)(2,1)}, bf16[2,256,512]{2,1,0:T(8,128)(2,1)S(1)}, u32[]{:S(2)}, u32[]{:S(2)}) collective-permute-start(bf16[2,256,512]{2,1,0:T(8,128)(2,1)} %collective-permute-done.35.refs_3_), channel_id=1, source_target_pairs={{0,32},{1,33},{2,34},{3,35},{4,36},{5,37},{6,38},{7,39},{8,40},{9,... | collective-permute-start | bytes 1572872 | tf_op jit(solution)/shard_map/ppermute | solution.py:43
  68.0 25.4 %collective-permute-start.24 = (bf16[256,256]{1,0:T(8,128)(2,1)S(1)}, bf16[256,256]{1,0:T(8,128)(2,1)S(1)}, u32[]{:S(2)}, u32[]{:S(2)}) collective-permute-start(bf16[256,256]{1,0:T(8,128)(2,1)S(1)} %slice_bitcast_fusion.2), channel_id=1, source_target_pairs={{0,32},{1,33},{2,34},{3,35},{4,36},{5,37},{6,38},{7,39},{8,40},{9,... | collective-permute-start | bytes 393224 | tf_op jit(solution)/shard_map/ppermute | solution.py:43
  70.1 11.7 %collective-permute-start.10 = (bf16[6,256,768]{2,1,0:T(8,128)(2,1)S(1)}, bf16[6,256,768]{2,1,0:T(8,128)(2,1)S(1)}, u32[]{:S(2)}, u32[]{:S(2)}) collective-permute-start(bf16[6,256,768]{2,1,0:T(8,128)(2,1)S(1)} %pad_maximum_fusion), channel_id=1, source_target_pairs={{0,16},{1,17},{2,18},{3,19},{4,20},{5,21},{6,22},{7,23},{8,24},{9,... | collective-permute-start | bytes 7077896 | tf_op jit(solution)/shard_map/ppermute | solution.py:43
  74.0 13.4 %collective-permute-start.12 = (bf16[256,768]{1,0:T(8,128)(2,1)S(1)}, bf16[256,768]{1,0:T(8,128)(2,1)S(1)}, u32[]{:S(2)}, u32[]{:S(2)}) collective-permute-start(bf16[256,768]{1,0:T(8,128)(2,1)S(1)} %collective-permute-done.11.far), channel_id=1, source_target_pairs={{0,16},{1,17},{2,18},{3,19},{4,20},{5,21},{6,22},{7,23},{8,24},{9,... | collective-permute-start | bytes 1179656 | tf_op jit(solution)/shard_map/ppermute | solution.py:43
  81.2 21.2 %collective-permute-start.37 = (bf16[2,256,512]{2,1,0:T(8,128)(2,1)S(1)}, bf16[2,256,512]{2,1,0:T(8,128)(2,1)S(1)}, u32[]{:S(2)}, u32[]{:S(2)}) collective-permute-start(bf16[2,256,512]{2,1,0:T(8,128)(2,1)S(1)} %collective-permute-done.36.refs_4_), channel_id=1, source_target_pairs={{0,32},{1,33},{2,34},{3,35},{4,36},{5,37},{6,38},{7,39},{8,40},{9,... | collective-permute-start | bytes 1572872 | tf_op jit(solution)/shard_map/ppermute | solution.py:43
  93.6 20.8 %collective-permute-start.25 = (bf16[7,256,256]{2,1,0:T(8,128)(2,1)S(1)}, bf16[7,256,256]{2,1,0:T(8,128)(2,1)S(1)}, u32[]{:S(2)}, u32[]{:S(2)}) collective-permute-start(bf16[7,256,256]{2,1,0:T(8,128)(2,1)S(1)} %pad_maximum_fusion.4), channel_id=1, source_target_pairs={{0,16},{1,17},{2,18},{3,19},{4,20},{5,21},{6,22},{7,23},{8,24},{9,... | collective-permute-start | bytes 2752520 | tf_op jit(solution)/shard_map/ppermute | solution.py:43
  103.0 19.2 %collective-permute-start.26 = (bf16[2,512,256]{2,1,0:T(8,128)(2,1)S(1)}, bf16[2,512,256]{2,1,0:T(8,128)(2,1)S(1)}, u32[]{:S(2)}, u32[]{:S(2)}) collective-permute-start(bf16[2,512,256]{2,1,0:T(8,128)(2,1)S(1)} %pad_maximum_fusion.7.refs_1_), channel_id=1, source_target_pairs={{0,1},{1,2},{2,3},{3,0},{4,5},{5,6},{6,7},{7,4},{8,9},{9,10},{10,1... | collective-permute-start | bytes 1572872 | tf_op jit(solution)/shard_map/ppermute | solution.py:43
  108.0 14.3 %collective-permute-start.27 = (bf16[2,512,256]{2,1,0:T(8,128)(2,1)S(1)}, bf16[2,512,256]{2,1,0:T(8,128)(2,1)S(1)}, u32[]{:S(2)}, u32[]{:S(2)}) collective-permute-start(bf16[2,512,256]{2,1,0:T(8,128)(2,1)S(1)} %pad_maximum_fusion.6.refs_0_), channel_id=1, source_target_pairs={{0,3},{1,0},{2,1},{3,2},{4,7},{5,4},{6,5},{7,6},{8,11},{9,8},{10,9... | collective-permute-start | bytes 1572872 | tf_op jit(solution)/shard_map/ppermute | solution.py:43
  110.4 15.0 %collective-permute-start.19 = (bf16[2,512,256]{2,1,0:T(8,128)(2,1)S(1)}, bf16[2,512,256]{2,1,0:T(8,128)(2,1)S(1)}, u32[]{:S(2)}, u32[]{:S(2)}) collective-permute-start(bf16[2,512,256]{2,1,0:T(8,128)(2,1)S(1)} %collective-permute-done.18.refs_5_), channel_id=1, source_target_pairs={{0,3},{1,0},{2,1},{3,2},{4,7},{5,4},{6,5},{7,6},{8,11},{9,8},{10,9... | collective-permute-start | bytes 1572872 | tf_op jit(solution)/shard_map/ppermute | solution.py:43
  111.6 13.8 %collective-permute-start.15 = (bf16[2,512,256]{2,1,0:T(8,128)(2,1)S(1)}, bf16[2,512,256]{2,1,0:T(8,128)(2,1)S(1)}, u32[]{:S(2)}, u32[]{:S(2)}) collective-permute-start(bf16[2,512,256]{2,1,0:T(8,128)(2,1)S(1)} %collective-permute-done.14.refs_2_), channel_id=1, source_target_pairs={{0,1},{1,2},{2,3},{3,0},{4,5},{5,6},{6,7},{7,4},{8,9},{9,10},{10,1... | collective-permute-start | bytes 1572872 | tf_op jit(solution)/shard_map/ppermute | solution.py:43
  115.3 41.3 %collective-permute-start.39 = (bf16[7,256,512]{2,1,0:T(8,128)(2,1)}, bf16[7,256,512]{2,1,0:T(8,128)(2,1)}, u32[]{:S(2)}, u32[]{:S(2)}) collective-permute-start(bf16[7,256,512]{2,1,0:T(8,128)(2,1)} %pad_maximum_fusion.1), channel_id=1, source_target_pairs={{0,16},{1,17},{2,18},{3,19},{4,20},{5,21},{6,22},{7,23},{8,24},{9,... | collective-permute-start | bytes 5505032 | tf_op jit(solution)/shard_map/ppermute | solution.py:43
  138.4 15.2 %collective-permute-start.31 = (bf16[4,512,256]{2,1,0:T(8,128)(2,1)S(1)}, bf16[4,512,256]{2,1,0:T(8,128)(2,1)S(1)}, u32[]{:S(2)}, u32[]{:S(2)}) collective-permute-start(bf16[4,512,256]{2,1,0:T(8,128)(2,1)S(1)} %pad_maximum_fusion.3.refs_0_), channel_id=1, source_target_pairs={{0,1},{1,2},{2,3},{3,0},{4,5},{5,6},{6,7},{7,4},{8,9},{9,10},{10,1... | collective-permute-start | bytes 3145736 | tf_op jit(solution)/shard_map/ppermute | solution.py:43
  138.5 15.3 %collective-permute-start.33 = (bf16[4,512,256]{2,1,0:T(8,128)(2,1)S(1)}, bf16[4,512,256]{2,1,0:T(8,128)(2,1)S(1)}, u32[]{:S(2)}, u32[]{:S(2)}) collective-permute-start(bf16[4,512,256]{2,1,0:T(8,128)(2,1)S(1)} %pad_maximum_fusion.3.refs_0_), channel_id=1, source_target_pairs={{0,3},{1,0},{2,1},{3,2},{4,7},{5,4},{6,5},{7,6},{8,11},{9,8},{10,9... | collective-permute-start | bytes 3145736 | tf_op jit(solution)/shard_map/ppermute | solution.py:43
  153.7 12.5 %collective-permute-start.32 = (bf16[2,512,256]{2,1,0:T(8,128)(2,1)S(1)}, bf16[2,512,256]{2,1,0:T(8,128)(2,1)S(1)}, u32[]{:S(2)}, u32[]{:S(2)}) collective-permute-start(bf16[2,512,256]{2,1,0:T(8,128)(2,1)S(1)} %slice.37), channel_id=1, source_target_pairs={{0,1},{1,2},{2,3},{3,0},{4,5},{5,6},{6,7},{7,4},{8,9},{9,10},{10,1... | collective-permute-start | bytes 1572872 | tf_op jit(solution)/shard_map/ppermute | solution.py:43
  153.9 12.3 %collective-permute-start.34 = (bf16[2,512,256]{2,1,0:T(8,128)(2,1)S(1)}, bf16[2,512,256]{2,1,0:T(8,128)(2,1)S(1)}, u32[]{:S(2)}, u32[]{:S(2)}) collective-permute-start(bf16[2,512,256]{2,1,0:T(8,128)(2,1)S(1)} %slice.38), channel_id=1, source_target_pairs={{0,3},{1,0},{2,1},{3,2},{4,7},{5,4},{6,5},{7,6},{8,11},{9,8},{10,9... | collective-permute-start | bytes 1572872 | tf_op jit(solution)/shard_map/ppermute | solution.py:43
  (37 other events, 373.1 us)

commit v3 on v1

--- a/solution.py
+++ b/solution.py
@@ -200,10 +200,10 @@
     wait_all(copies)
     weight = held.reshape(14 * HD, 3 * HD)
 
-    @pl.loop(0, 12)
+    @pl.loop(0, 6)
     def _(n):
-        here = pl.ds(pl.multiple_of(lax.rem(n, 4) * 128, 128), 128)
-        there = pl.ds(pl.multiple_of(lax.div(n, 4) * HD, HD), HD)
+        here = pl.ds(pl.multiple_of(lax.div(n, 3) * PLEN, PLEN), PLEN)
+        there = pl.ds(pl.multiple_of(lax.rem(n, 3) * HD, HD), HD)
         total[here, there] = jnp.dot(
             rows[here, : 14 * HD], weight[:, there], preferred_element_type=jnp.float32
         )
@@ -215,15 +215,12 @@
         here = pl.ds(pl.multiple_of(p * PLEN, PLEN), PLEN)
         mean = jnp.sum(square[here, :], axis=1, keepdims=True) / D
         inverse = lax.rsqrt(mean + epsilon)
-
-        @pl.loop(0, 3)
-        def _(n):
-            there = pl.ds(pl.multiple_of(n * HD, HD), HD)
+        for n in range(3):
+            there = pl.ds(n * HD, HD)
             head = total[here, there]
             head += jnp.dot(rows[here, 14 * HD : 15 * HD], far[:, there], preferred_element_type=jnp.float32)
             head += jnp.dot(rows[here, 15 * HD :], far_crossed[:, there], preferred_element_type=jnp.float32)
             heads[n] = (head * inverse).astype(jnp.bfloat16)
-
         scores = lax.dot_general(
             heads[0], heads[1], (((1,), (1,)), ((), ())), preferred_element_type=jnp.float32
         ) * HD ** (-0.5)
@@ -236,13 +233,15 @@
 
 def arrange_kernel(*refs):
     place = read(refs[0])
-    parts, out, sem = refs[1:8], refs[8], refs[9]
-    copies = []
-    for n, (part, spot, row) in enumerate(late_places(place)):
+    parts, out = refs[1:8], refs[8]
+    for part, spot, row in late_places(place):
         source = parts[part] if spot is None else parts[part].at[spot]
-        copies.append(pltpu.make_async_copy(source, out.at[gather_spot(place, row)], sem.at[n]))
-    start_all(copies)
-    wait_all(copies)
+        target = out.at[gather_spot(place, row)]
+
+        @pl.loop(0, HD // 64)
+        def _(tile):
+            here = pl.ds(pl.multiple_of(tile * 64, 64), 64)
+            target[here, :] = source[here, :]
 
 
 def residual_near_kernel(*refs):
@@ -262,9 +261,9 @@
     load.start()
     load.wait()
 
-    @pl.loop(0, 4)
+    @pl.loop(0, 2)
     def _(p):
-        here = pl.ds(pl.multiple_of(p * 128, 128), 128)
+        here = pl.ds(pl.multiple_of(p * PLEN, PLEN), PLEN)
         sum_here = total[here, :]
         for k in range(SIDE):
             part = (far_back, far_ahead)[k // 2]
@@ -318,7 +317,7 @@
     return jax.ShapeDtypeStruct(shape, jnp.float32)
 
 
-def call(kernel, outs, ins, scratch, flops, moved, grant=28):
+def call(kernel, outs, ins, scratch, flops, moved, grant=16):
     return pl.pallas_call(
         kernel,
         out_shape=outs,
@@ -379,7 +378,6 @@
     crossvalue_weight,
 ):
     tokens = 2 * PLEN
-    dma = pltpu.SemaphoreType.DMA((BLOCKS,))
     place = jnp.stack([lax.axis_index("row"), lax.axis_index("col")]).astype(jnp.int32)
     qkv_weight = side_by_side(query_weight, key_weight, value_weight)
     qkv_other = swap_cores(qkv_weight)
@@ -421,7 +419,7 @@
     def arrange(weight):
         width = weight[0].shape[1]
         return call(
-            arrange_kernel, bf16(BLOCKS, HD, width), [SMEM] + [ANY] * 7, [dma], 0, 4 * D * width
+            arrange_kernel, bf16(BLOCKS, HD, width), [SMEM] + [VMEM] * 7, [], 0, 4 * D * width
         )(place, *weight)
 
     near, far = gather_split(attended)

time: 168 us -> 165 us (0.982)
  Pallas kernels: 31.4 us -> 25.9 us
  waiting for transfers between devices: 66.8 us -> 69.4 us
    pallas_call x2, Pallas kernels: 5.5 us -> 2.58 us  [arrange(): call(arrange_kernel, bf16(BLOCKS, HD, width), [SMEM] + [VMEM] * 7, [], 0,...]
    ppermute x42, waiting for transfers between devices: 66.8 us -> 69.4 us  [send(): return lax.ppermute(block, ('row', 'col'), moves(step))]
  transfers between devices with their start and end apart: 42 -> 42, of which waited for: 18 -> 19; matrix products, arithmetic and copies ran while one was open for 7% -> 7% of each run, Pallas kernels for 16% -> 13%
where the time goes in v3:
time: 165 us
  waiting for transfers between devices  69.4 us (42%)
  starting transfers between devices  54.5 us (33%)
  Pallas kernels  25.9 us (16%)
  local copies, waits for them, and re-layouts  8.64 us (5%)
  other arithmetic  5.49 us (3%)
    ppermute x42, waiting for transfers between devices, send(): return lax.ppermute(block, ('row', 'col'), moves(step))  69.4 us
    ppermute x42, starting transfers between devices, send(): return lax.ppermute(block, ('row', 'col'), moves(step))  54.5 us
    gather x1, local copies, waits for them, and re-layouts, body(): embedded = embedding.at[token_ids.reshape(-1)].get(mode='promise_in_bounds')  6.31 us
    pallas_call x1, Pallas kernels, body(): call(project_kernel, f32(tokens, 3 * HD), [VMEM] + [ANY] * 6, [vmem(14, H...  5.56 us
    pallas_call x1, Pallas kernels, body(): call(prepare_kernel, (bf16(tokens, D), f32(tokens, 128), f32(BLOCKS, 1, H...  4.33 us
    pallas_call x2, Pallas kernels, side_by_side(): call(join_kernel, bf16(HD, len(shards) * HD), [HBM] * len(shards), [pltpu...  3.62 us
  transfers between devices with their start and end apart: 42, of which 19 were waited for; matrix products, arithmetic and copies ran while one was open for 7% of the time, Pallas kernels for 13%

profile of v3, /device:TPU:6, one launch (start us, length us, event | category | flops | bytes accessed | tf_op | source)
XLA Modules:
  0.0 165.3 jit_solution(1024531363429770352)
XLA Ops:
  9.5 3.9 %collective-permute-start.20 = (bf16[256,768]{1,0:T(8,128)(2,1)}, bf16[256,768]{1,0:T(8,128)(2,1)S(1)}, u32[]{:S(2)}, u32[]{:S(2)}) collective-permute-start(bf16[256,768]{1,0:T(8,128)(2,1)} %shard_map.135), channel_id=1, source_target_pairs={{0,16},{1,17},{2,18},{3,19},{4,20},{5,21},{6,22},{7,23},{8,24},{9,... | collective-permute-start | bytes 1179656 | tf_op jit(solution)/shard_map/ppermute | solution.py:43
  13.4 8.2 %collective-permute-done.7.hop1 = bf16[2,256,768]{2,1,0:T(8,128)(2,1)S(1)} collective-permute-done((bf16[2,256,768]{2,1,0:T(8,128)(2,1)S(1)}, bf16[2,256,768]{2,1,0:T(8,128)(2,1)S(1)}, u32[]{:S(2)}, u32[]{:S(2)}) %collective-permute-start.7) | collective-permute-done | bytes 786464 | tf_op jit(solution)/shard_map/ppermute | solution.py:43
  21.7 6.3 %gather_fusion = bf16[512,256]{1,0:T(8,128)(2,1)S(1)} fusion(bf16[16384,256]{1,0:T(8,128)(2,1)} %param.13, s32[1024]{0:T(1024)S(1)} %pad_clamp_fusion), kind=kCustom, calls=%fused_computation | custom fusion | bytes 526336 | tf_op jit(solution)/shard_map/gather | solution.py:385
  32.5 2.5 %collective-permute-done.8.hop2 = bf16[2,256,768]{2,1,0:T(8,128)(2,1)} collective-permute-done((bf16[2,256,768]{2,1,0:T(8,128)(2,1)S(1)}, bf16[2,256,768]{2,1,0:T(8,128)(2,1)}, u32[]{:S(2)}, u32[]{:S(2)}) %collective-permute-start.8) | collective-permute-done | bytes 786464 | tf_op jit(solution)/shard_map/ppermute | solution.py:43
  35.7 3.6 %collective-permute-done.21.refs_3_ = bf16[2,256,256]{2,1,0:T(8,128)(2,1)S(1)} collective-permute-done((bf16[2,256,256]{2,1,0:T(8,128)(2,1)S(1)}, bf16[2,256,256]{2,1,0:T(8,128)(2,1)S(1)}, u32[]{:S(2)}, u32[]{:S(2)}) %collective-permute-start.21) | collective-permute-done | bytes 262176 | tf_op jit(solution)/shard_map/ppermute | solution.py:43
  45.9 5.2 %collective-permute-done.22.refs_4_ = bf16[2,256,256]{2,1,0:T(8,128)(2,1)S(1)} collective-permute-done((bf16[2,256,256]{2,1,0:T(8,128)(2,1)S(1)}, bf16[2,256,256]{2,1,0:T(8,128)(2,1)S(1)}, u32[]{:S(2)}, u32[]{:S(2)}) %collective-permute-start.22) | collective-permute-done | bytes 262176 | tf_op jit(solution)/shard_map/ppermute | solution.py:43
  51.9 3.2 %collective-permute-start.5 = (bf16[4,528,256]{2,1,0:T(8,128)(2,1)S(1)}, bf16[4,528,256]{2,1,0:T(8,128)(2,1)}, u32[]{:S(2)}, u32[]{:S(2)}) collective-permute-start(bf16[4,528,256]{2,1,0:T(8,128)(2,1)S(1)} %pad_maximum_fusion.2.own), channel_id=1, source_target_pairs={{0,2},{1,3},{2,0},{3,1},{4,6},{5,7},{6,4},{7,5},{8,10},{9,11},{10,... | collective-permute-start | bytes 3244040 | tf_op jit(solution)/shard_map/ppermute | solution.py:43
  56.9 2.3 %collective-permute-start.36 = (bf16[2,256,512]{2,1,0:T(8,128)(2,1)S(1)}, bf16[2,256,512]{2,1,0:T(8,128)(2,1)S(1)}, u32[]{:S(2)}, u32[]{:S(2)}) collective-permute-start(bf16[2,256,512]{2,1,0:T(8,128)(2,1)S(1)} %collective-permute-done.35.refs_3_), channel_id=1, source_target_pairs={{0,32},{1,33},{2,34},{3,35},{4,36},{5,37},{6,38},{7,39},{8,40},{9,... | collective-permute-start | bytes 1572872 | tf_op jit(solution)/shard_map/ppermute | solution.py:43
  59.2 5.3 %collective-permute-done.23.refs_5_ = bf16[2,256,256]{2,1,0:T(8,128)(2,1)S(1)} collective-permute-done((bf16[2,256,256]{2,1,0:T(8,128)(2,1)}, bf16[2,256,256]{2,1,0:T(8,128)(2,1)S(1)}, u32[]{:S(2)}, u32[]{:S(2)}) %collective-permute-start.23) | collective-permute-done | bytes 262176 | tf_op jit(solution)/shard_map/ppermute | solution.py:43
  67.4 2.4 %collective-permute-start.10 = (bf16[6,256,768]{2,1,0:T(8,128)(2,1)S(1)}, bf16[6,256,768]{2,1,0:T(8,128)(2,1)S(1)}, u32[]{:S(2)}, u32[]{:S(2)}) collective-permute-start(bf16[6,256,768]{2,1,0:T(8,128)(2,1)S(1)} %pad_maximum_fusion), channel_id=1, source_target_pairs={{0,16},{1,17},{2,18},{3,19},{4,20},{5,21},{6,22},{7,23},{8,24},{9,... | collective-permute-start | bytes 7077896 | tf_op jit(solution)/shard_map/ppermute | solution.py:43
  69.8 4.6 %collective-permute-done.11.far = bf16[256,768]{1,0:T(8,128)(2,1)S(1)} collective-permute-done((bf16[256,768]{1,0:T(8,128)(2,1)S(1)}, bf16[256,768]{1,0:T(8,128)(2,1)S(1)}, u32[]{:S(2)}, u32[]{:S(2)}) %collective-permute-start.11) | collective-permute-done | bytes 393248 | tf_op jit(solution)/shard_map/ppermute | solution.py:43
  74.4 4.3 %shard_map.131 = (bf16[512,4096]{1,0:T(8,128)(2,1)S(1)}, f32[512,128]{1,0:T(8,128)S(1)}, f32[16,1,256]{2,1,0:T(1,128)S(1)}) custom-call(s32[2]{0:T(128)S(1)} %pad_add_fusion.place_ref.refs_0_, bf16[4,528,256]{2,1,0:T(8,128)(2,1)S(1)} %pad_maximum_fusion.2.own, bf16[4,528,256]{2,1,0:T(8,128)(2,1)} %collective-permute-done.3.back, ...), custom_call_target="tpu_custom_call" | custom-call | flops 53687091200 | bytes 8388608 | tf_op jit(solution)/shard_map/pallas_call | solution.py:390
  78.8 5.6 %shard_map.133.total = f32[512,768]{1,0:T(8,128)S(1)} custom-call(bf16[512,4096]{1,0:T(8,128)(2,1)S(1)} %get-tuple-element.10.rows, bf16[256,768]{1,0:T(8,128)(2,1)S(1)} %copy-done, bf16[256,768]{1,0:T(8,128)(2,1)S(1)} %copy-done.11, bf16[2,256,768]{2,1,0:T(8,128)(2,1)S(1)} %copy-done.9, bf16[2,256,768]{2,1,0:T(8,128)(2,1)} %collective-permute-done.8.hop2, ...), custom_call_target="tpu_custom_call" | custom-call | flops 3221225472 | bytes 10485760 | tf_op jit(solution)/shard_map/pallas_call | solution.py:398
  91.7 5.3 %collective-permute-done.16 = bf16[512,256]{1,0:T(8,128)(2,1)S(1)} collective-permute-done((bf16[512,256]{1,0:T(8,128)(2,1)S(1)}, bf16[512,256]{1,0:T(8,128)(2,1)S(1)}, u32[]{:S(2)}, u32[]{:S(2)}) %collective-permute-start.16) | collective-permute-done | bytes 262176 | tf_op jit(solution)/shard_map/ppermute | solution.py:43
  97.1 3.1 %collective-permute-start.18 = (bf16[2,512,256]{2,1,0:T(8,128)(2,1)S(1)}, bf16[2,512,256]{2,1,0:T(8,128)(2,1)S(1)}, u32[]{:S(2)}, u32[]{:S(2)}) collective-permute-start(bf16[2,512,256]{2,1,0:T(8,128)(2,1)S(1)} %pad_maximum_fusion.6.refs_1_), channel_id=1, source_target_pairs={{0,3},{1,0},{2,1},{3,2},{4,7},{5,4},{6,5},{7,6},{8,11},{9,8},{10,9... | collective-permute-start | bytes 1572872 | tf_op jit(solution)/shard_map/ppermute | solution.py:43
  102.0 6.1 %collective-permute-done.38.refs_6_ = bf16[256,512]{1,0:T(8,128)(2,1)S(1)} collective-permute-done((bf16[256,512]{1,0:T(8,128)(2,1)S(1)}, bf16[256,512]{1,0:T(8,128)(2,1)S(1)}, u32[]{:S(2)}, u32[]{:S(2)}) %collective-permute-start.38) | collective-permute-done | bytes 262176 | tf_op jit(solution)/shard_map/ppermute | solution.py:43
  108.1 3.2 %collective-permute-start.27 = (bf16[2,512,256]{2,1,0:T(8,128)(2,1)S(1)}, bf16[2,512,256]{2,1,0:T(8,128)(2,1)S(1)}, u32[]{:S(2)}, u32[]{:S(2)}) collective-permute-start(bf16[2,512,256]{2,1,0:T(8,128)(2,1)S(1)} %pad_maximum_fusion.5.refs_0_), channel_id=1, source_target_pairs={{0,3},{1,0},{2,1},{3,2},{4,7},{5,4},{6,5},{7,6},{8,11},{9,8},{10,9... | collective-permute-start | bytes 1572872 | tf_op jit(solution)/shard_map/ppermute | solution.py:43
  119.5 4.1 %collective-permute-done.19.far_ahead = bf16[2,512,256]{2,1,0:T(8,128)(2,1)S(1)} collective-permute-done((bf16[2,512,256]{2,1,0:T(8,128)(2,1)S(1)}, bf16[2,512,256]{2,1,0:T(8,128)(2,1)S(1)}, u32[]{:S(2)}, u32[]{:S(2)}) %collective-permute-start.19) | collective-permute-done | bytes 524320 | tf_op jit(solution)/shard_map/ppermute | solution.py:43
  129.1 6.1 %collective-permute-done.31 = bf16[512,256]{1,0:T(8,128)(2,1)S(1)} collective-permute-done((bf16[512,256]{1,0:T(8,128)(2,1)}, bf16[512,256]{1,0:T(8,128)(2,1)S(1)}, u32[]{:S(2)}, u32[]{:S(2)}) %collective-permute-start.31) | collective-permute-done | bytes 262176 | tf_op jit(solution)/shard_map/ppermute | solution.py:43
  136.2 4.0 %collective-permute-start.33 = (bf16[2,512,256]{2,1,0:T(8,128)(2,1)S(1)}, bf16[2,512,256]{2,1,0:T(8,128)(2,1)S(1)}, u32[]{:S(2)}, u32[]{:S(2)}) collective-permute-start(bf16[2,512,256]{2,1,0:T(8,128)(2,1)S(1)} %pad_maximum_fusion.8.refs_1_), channel_id=1, source_target_pairs={{0,3},{1,0},{2,1},{3,2},{4,7},{5,4},{6,5},{7,6},{8,11},{9,8},{10,9... | collective-permute-start | bytes 1572872 | tf_op jit(solution)/shard_map/ppermute | solution.py:43
  146.9 3.7 %collective-permute-start.34 = (bf16[2,512,256]{2,1,0:T(8,128)(2,1)S(1)}, bf16[2,512,256]{2,1,0:T(8,128)(2,1)S(1)}, u32[]{:S(2)}, u32[]{:S(2)}) collective-permute-start(bf16[2,512,256]{2,1,0:T(8,128)(2,1)S(1)} %collective-permute-done.33.refs_5_), channel_id=1, source_target_pairs={{0,3},{1,0},{2,1},{3,2},{4,7},{5,4},{6,5},{7,6},{8,11},{9,8},{10,9... | collective-permute-start | bytes 1572872 | tf_op jit(solution)/shard_map/ppermute | solution.py:43
  153.1 4.2 %collective-permute-done.40.refs_3_ = bf16[2,512,256]{2,1,0:T(8,128)(2,1)S(1)} collective-permute-done((bf16[2,512,256]{2,1,0:T(8,128)(2,1)S(1)}, bf16[2,512,256]{2,1,0:T(8,128)(2,1)S(1)}, u32[]{:S(2)}, u32[]{:S(2)}) %collective-permute-start.40) | collective-permute-done | bytes 524320 | tf_op jit(solution)/shard_map/ppermute | solution.py:43
  157.3 2.6 %shard_map.140 = (f32[512,512]{1,0:T(8,128)S(1)}, f32[512,128]{1,0:T(8,128)S(1)}) custom-call(bf16[2,512,256]{2,1,0:T(8,128)(2,1)S(1)} %pad_maximum_fusion.7.refs_0_, bf16[2,512,256]{2,1,0:T(8,128)(2,1)S(1)} %pad_maximum_fusion.8.refs_1_, bf16[2,512,256]{2,1,0:T(8,128)(2,1)S(1)} %collective-permute-done.29.refs_2_, ...), custom_call_target="tpu_custom_call" | custom-call | flops 2147483648 | bytes 8388608 | tf_op jit(solution)/shard_map/pallas_call | solution.py:440
  159.9 3.0 %collective-permute-done.30.far_back = bf16[2,512,256]{2,1,0:T(8,128)(2,1)S(1)} collective-permute-done((bf16[2,512,256]{2,1,0:T(8,128)(2,1)S(1)}, bf16[2,512,256]{2,1,0:T(8,128)(2,1)S(1)}, u32[]{:S(2)}, u32[]{:S(2)}) %collective-permute-start.30) | collective-permute-done | bytes 524320 | tf_op jit(solution)/shard_map/ppermute | solution.py:43
  (128 shorter events, 61.1 us)
Async XLA Ops:
  5.7 15.9 %collective-permute-start.7 = (bf16[2,256,768]{2,1,0:T(8,128)(2,1)S(1)}, bf16[2,256,768]{2,1,0:T(8,128)(2,1)S(1)}, u32[]{:S(2)}, u32[]{:S(2)}) collective-permute-start(bf16[2,256,768]{2,1,0:T(8,128)(2,1)S(1)} %pad_maximum_fusion.4), channel_id=1, source_target_pairs={{0,32},{1,33},{2,34},{3,35},{4,36},{5,37},{6,38},{7,39},{8,40},{9,... | collective-permute-start | bytes 2359304 | tf_op jit(solution)/shard_map/ppermute | solution.py:43
  9.5 22.0 %collective-permute-start.20 = (bf16[256,768]{1,0:T(8,128)(2,1)}, bf16[256,768]{1,0:T(8,128)(2,1)S(1)}, u32[]{:S(2)}, u32[]{:S(2)}) collective-permute-start(bf16[256,768]{1,0:T(8,128)(2,1)} %shard_map.135), channel_id=1, source_target_pairs={{0,16},{1,17},{2,18},{3,19},{4,20},{5,21},{6,22},{7,23},{8,24},{9,... | collective-permute-start | bytes 1179656 | tf_op jit(solution)/shard_map/ppermute | solution.py:43
  21.6 13.3 %collective-permute-start.8 = (bf16[2,256,768]{2,1,0:T(8,128)(2,1)S(1)}, bf16[2,256,768]{2,1,0:T(8,128)(2,1)}, u32[]{:S(2)}, u32[]{:S(2)}) collective-permute-start(bf16[2,256,768]{2,1,0:T(8,128)(2,1)S(1)} %collective-permute-done.7.hop1), channel_id=1, source_target_pairs={{0,32},{1,33},{2,34},{3,35},{4,36},{5,37},{6,38},{7,39},{8,40},{9,... | collective-permute-start | bytes 2359304 | tf_op jit(solution)/shard_map/ppermute | solution.py:43
  28.0 12.1 %collective-permute-start = (bf16[528,256]{1,0:T(8,128)(2,1)S(1)}, bf16[528,256]{1,0:T(8,128)(2,1)S(1)}, u32[]{:S(2)}, u32[]{:S(2)}) collective-permute-start(bf16[528,256]{1,0:T(8,128)(2,1)S(1)} %shard_map.130), channel_id=1, source_target_pairs={{0,4},{1,5},{2,6},{3,7},{4,8},{5,9},{6,10},{7,11},{8,12},{9,13},{1... | collective-permute-start | bytes 811016 | tf_op jit(solution)/shard_map/ppermute | solution.py:43
  28.6 13.9 %collective-permute-start.1 = (bf16[528,256]{1,0:T(8,128)(2,1)S(1)}, bf16[528,256]{1,0:T(8,128)(2,1)S(1)}, u32[]{:S(2)}, u32[]{:S(2)}) collective-permute-start(bf16[528,256]{1,0:T(8,128)(2,1)S(1)} %shard_map.130), channel_id=1, source_target_pairs={{0,12},{1,13},{2,14},{3,15},{4,0},{5,1},{6,2},{7,3},{8,4},{9,5},{1... | collective-permute-start | bytes 811016 | tf_op jit(solution)/shard_map/ppermute | solution.py:43
  30.1 12.3 %collective-permute-start.2 = (bf16[528,256]{1,0:T(8,128)(2,1)S(1)}, bf16[528,256]{1,0:T(8,128)(2,1)S(1)}, u32[]{:S(2)}, u32[]{:S(2)}) collective-permute-start(bf16[528,256]{1,0:T(8,128)(2,1)S(1)} %shard_map.130), channel_id=1, source_target_pairs={{0,8},{1,9},{2,10},{3,11},{4,12},{5,13},{6,14},{7,15},{8,0},{9,1},... | collective-permute-start | bytes 811016 | tf_op jit(solution)/shard_map/ppermute | solution.py:43
  34.9 21.9 %collective-permute-start.9 = (bf16[2,256,768]{2,1,0:T(8,128)(2,1)}, bf16[2,256,768]{2,1,0:T(8,128)(2,1)S(1)}, u32[]{:S(2)}, u32[]{:S(2)}) collective-permute-start(bf16[2,256,768]{2,1,0:T(8,128)(2,1)} %collective-permute-done.8.hop2), channel_id=1, source_target_pairs={{0,32},{1,33},{2,34},{3,35},{4,36},{5,37},{6,38},{7,39},{8,40},{9,... | collective-permute-start | bytes 2359304 | tf_op jit(solution)/shard_map/ppermute | solution.py:43
  39.3 11.9 %collective-permute-start.22 = (bf16[2,256,256]{2,1,0:T(8,128)(2,1)S(1)}, bf16[2,256,256]{2,1,0:T(8,128)(2,1)S(1)}, u32[]{:S(2)}, u32[]{:S(2)}) collective-permute-start(bf16[2,256,256]{2,1,0:T(8,128)(2,1)S(1)} %collective-permute-done.21.refs_3_), channel_id=1, source_target_pairs={{0,32},{1,33},{2,34},{3,35},{4,36},{5,37},{6,38},{7,39},{8,40},{9,... | collective-permute-start | bytes 786440 | tf_op jit(solution)/shard_map/ppermute | solution.py:43
  40.2 16.6 %collective-permute-start.35 = (bf16[2,256,512]{2,1,0:T(8,128)(2,1)}, bf16[2,256,512]{2,1,0:T(8,128)(2,1)S(1)}, u32[]{:S(2)}, u32[]{:S(2)}) collective-permute-start(bf16[2,256,512]{2,1,0:T(8,128)(2,1)} %pad_maximum_fusion.9), channel_id=1, source_target_pairs={{0,32},{1,33},{2,34},{3,35},{4,36},{5,37},{6,38},{7,39},{8,40},{9,... | collective-permute-start | bytes 1572872 | tf_op jit(solution)/shard_map/ppermute | solution.py:43
  42.6 23.6 %collective-permute-start.3 = (bf16[4,528,256]{2,1,0:T(8,128)(2,1)S(1)}, bf16[4,528,256]{2,1,0:T(8,128)(2,1)}, u32[]{:S(2)}, u32[]{:S(2)}) collective-permute-start(bf16[4,528,256]{2,1,0:T(8,128)(2,1)S(1)} %pad_maximum_fusion.2.own), channel_id=1, source_target_pairs={{0,1},{1,2},{2,3},{3,0},{4,5},{5,6},{6,7},{7,4},{8,9},{9,10},{10,1... | collective-permute-start | bytes 3244040 | tf_op jit(solution)/shard_map/ppermute | solution.py:43
  44.3 23.2 %collective-permute-start.4 = (bf16[4,528,256]{2,1,0:T(8,128)(2,1)S(1)}, bf16[4,528,256]{2,1,0:T(8,128)(2,1)}, u32[]{:S(2)}, u32[]{:S(2)}) collective-permute-start(bf16[4,528,256]{2,1,0:T(8,128)(2,1)S(1)} %pad_maximum_fusion.2.own), channel_id=1, source_target_pairs={{0,3},{1,0},{2,1},{3,2},{4,7},{5,4},{6,5},{7,6},{8,11},{9,8},{10,9... | collective-permute-start | bytes 3244040 | tf_op jit(solution)/shard_map/ppermute | solution.py:43
  51.9 22.5 %collective-permute-start.5 = (bf16[4,528,256]{2,1,0:T(8,128)(2,1)S(1)}, bf16[4,528,256]{2,1,0:T(8,128)(2,1)}, u32[]{:S(2)}, u32[]{:S(2)}) collective-permute-start(bf16[4,528,256]{2,1,0:T(8,128)(2,1)S(1)} %pad_maximum_fusion.2.own), channel_id=1, source_target_pairs={{0,2},{1,3},{2,0},{3,1},{4,6},{5,7},{6,4},{7,5},{8,10},{9,11},{10,... | collective-permute-start | bytes 3244040 | tf_op jit(solution)/shard_map/ppermute | solution.py:43
  56.9 32.8 %collective-permute-start.36 = (bf16[2,256,512]{2,1,0:T(8,128)(2,1)S(1)}, bf16[2,256,512]{2,1,0:T(8,128)(2,1)S(1)}, u32[]{:S(2)}, u32[]{:S(2)}) collective-permute-start(bf16[2,256,512]{2,1,0:T(8,128)(2,1)S(1)} %collective-permute-done.35.refs_3_), channel_id=1, source_target_pairs={{0,32},{1,33},{2,34},{3,35},{4,36},{5,37},{6,38},{7,39},{8,40},{9,... | collective-permute-start | bytes 1572872 | tf_op jit(solution)/shard_map/ppermute | solution.py:43
  66.3 25.2 %collective-permute-start.24 = (bf16[256,256]{1,0:T(8,128)(2,1)S(1)}, bf16[256,256]{1,0:T(8,128)(2,1)S(1)}, u32[]{:S(2)}, u32[]{:S(2)}) collective-permute-start(bf16[256,256]{1,0:T(8,128)(2,1)S(1)} %slice_bitcast_fusion.2), channel_id=1, source_target_pairs={{0,32},{1,33},{2,34},{3,35},{4,36},{5,37},{6,38},{7,39},{8,40},{9,... | collective-permute-start | bytes 393224 | tf_op jit(solution)/shard_map/ppermute | solution.py:43
  91.6 21.9 %collective-permute-start.25 = (bf16[7,256,256]{2,1,0:T(8,128)(2,1)S(1)}, bf16[7,256,256]{2,1,0:T(8,128)(2,1)S(1)}, u32[]{:S(2)}, u32[]{:S(2)}) collective-permute-start(bf16[7,256,256]{2,1,0:T(8,128)(2,1)S(1)} %pad_maximum_fusion.3), channel_id=1, source_target_pairs={{0,16},{1,17},{2,18},{3,19},{4,20},{5,21},{6,22},{7,23},{8,24},{9,... | collective-permute-start | bytes 2752520 | tf_op jit(solution)/shard_map/ppermute | solution.py:43
  97.1 14.2 %collective-permute-start.18 = (bf16[2,512,256]{2,1,0:T(8,128)(2,1)S(1)}, bf16[2,512,256]{2,1,0:T(8,128)(2,1)S(1)}, u32[]{:S(2)}, u32[]{:S(2)}) collective-permute-start(bf16[2,512,256]{2,1,0:T(8,128)(2,1)S(1)} %pad_maximum_fusion.6.refs_1_), channel_id=1, source_target_pairs={{0,3},{1,0},{2,1},{3,2},{4,7},{5,4},{6,5},{7,6},{8,11},{9,8},{10,9... | collective-permute-start | bytes 1572872 | tf_op jit(solution)/shard_map/ppermute | solution.py:43
  100.5 15.9 %collective-permute-start.26 = (bf16[2,512,256]{2,1,0:T(8,128)(2,1)S(1)}, bf16[2,512,256]{2,1,0:T(8,128)(2,1)S(1)}, u32[]{:S(2)}, u32[]{:S(2)}) collective-permute-start(bf16[2,512,256]{2,1,0:T(8,128)(2,1)S(1)} %pad_maximum_fusion.6.refs_1_), channel_id=1, source_target_pairs={{0,1},{1,2},{2,3},{3,0},{4,5},{5,6},{6,7},{7,4},{8,9},{9,10},{10,1... | collective-permute-start | bytes 1572872 | tf_op jit(solution)/shard_map/ppermute | solution.py:43
  111.3 12.3 %collective-permute-start.19 = (bf16[2,512,256]{2,1,0:T(8,128)(2,1)S(1)}, bf16[2,512,256]{2,1,0:T(8,128)(2,1)S(1)}, u32[]{:S(2)}, u32[]{:S(2)}) collective-permute-start(bf16[2,512,256]{2,1,0:T(8,128)(2,1)S(1)} %collective-permute-done.18.refs_5_), channel_id=1, source_target_pairs={{0,3},{1,0},{2,1},{3,2},{4,7},{5,4},{6,5},{7,6},{8,11},{9,8},{10,9... | collective-permute-start | bytes 1572872 | tf_op jit(solution)/shard_map/ppermute | solution.py:43
  111.4 12.1 %collective-permute-start.15 = (bf16[2,512,256]{2,1,0:T(8,128)(2,1)S(1)}, bf16[2,512,256]{2,1,0:T(8,128)(2,1)S(1)}, u32[]{:S(2)}, u32[]{:S(2)}) collective-permute-start(bf16[2,512,256]{2,1,0:T(8,128)(2,1)S(1)} %collective-permute-done.14.refs_2_), channel_id=1, source_target_pairs={{0,1},{1,2},{2,3},{3,0},{4,5},{5,6},{6,7},{7,4},{8,9},{9,10},{10,1... | collective-permute-start | bytes 1572872 | tf_op jit(solution)/shard_map/ppermute | solution.py:43
  113.6 38.1 %collective-permute-start.39 = (bf16[7,256,512]{2,1,0:T(8,128)(2,1)S(1)}, bf16[7,256,512]{2,1,0:T(8,128)(2,1)S(1)}, u32[]{:S(2)}, u32[]{:S(2)}) collective-permute-start(bf16[7,256,512]{2,1,0:T(8,128)(2,1)S(1)} %pad_maximum_fusion.1), channel_id=1, source_target_pairs={{0,16},{1,17},{2,18},{3,19},{4,20},{5,21},{6,22},{7,23},{8,24},{9,... | collective-permute-start | bytes 5505032 | tf_op jit(solution)/shard_map/ppermute | solution.py:43
  127.7 12.5 %collective-permute-start.28 = (bf16[512,256]{1,0:T(8,128)(2,1)}, bf16[512,256]{1,0:T(8,128)(2,1)S(1)}, u32[]{:S(2)}, u32[]{:S(2)}) collective-permute-start(bf16[512,256]{1,0:T(8,128)(2,1)} %shard_map.138), channel_id=1, source_target_pairs={{0,4},{1,5},{2,6},{3,7},{4,8},{5,9},{6,10},{7,11},{8,12},{9,13},{1... | collective-permute-start | bytes 786440 | tf_op jit(solution)/shard_map/ppermute | solution.py:43
  141.3 16.0 %collective-permute-start.40 = (bf16[2,512,256]{2,1,0:T(8,128)(2,1)S(1)}, bf16[2,512,256]{2,1,0:T(8,128)(2,1)S(1)}, u32[]{:S(2)}, u32[]{:S(2)}) collective-permute-start(bf16[2,512,256]{2,1,0:T(8,128)(2,1)S(1)} %pad_maximum_fusion.8.refs_1_), channel_id=1, source_target_pairs={{0,1},{1,2},{2,3},{3,0},{4,5},{5,6},{6,7},{7,4},{8,9},{9,10},{10,1... | collective-permute-start | bytes 1572872 | tf_op jit(solution)/shard_map/ppermute | solution.py:43
  142.7 14.6 %collective-permute-start.41 = (bf16[2,512,256]{2,1,0:T(8,128)(2,1)S(1)}, bf16[2,512,256]{2,1,0:T(8,128)(2,1)S(1)}, u32[]{:S(2)}, u32[]{:S(2)}) collective-permute-start(bf16[2,512,256]{2,1,0:T(8,128)(2,1)S(1)} %pad_maximum_fusion.7.refs_0_), channel_id=1, source_target_pairs={{0,3},{1,0},{2,1},{3,2},{4,7},{5,4},{6,5},{7,6},{8,11},{9,8},{10,9... | collective-permute-start | bytes 1572872 | tf_op jit(solution)/shard_map/ppermute | solution.py:43
  146.9 13.0 %collective-permute-start.34 = (bf16[2,512,256]{2,1,0:T(8,128)(2,1)S(1)}, bf16[2,512,256]{2,1,0:T(8,128)(2,1)S(1)}, u32[]{:S(2)}, u32[]{:S(2)}) collective-permute-start(bf16[2,512,256]{2,1,0:T(8,128)(2,1)S(1)} %collective-permute-done.33.refs_5_), channel_id=1, source_target_pairs={{0,3},{1,0},{2,1},{3,2},{4,7},{5,4},{6,5},{7,6},{8,11},{9,8},{10,9... | collective-permute-start | bytes 1572872 | tf_op jit(solution)/shard_map/ppermute | solution.py:43
  (35 other events, 412.3 us)
